TPU v7x, 32 devices: a whole 2x2x4 slice. The times are simulated.
32 devices in a mesh: groups: 2 (over x), pages: 16 (over z, y, core).
Axes of the slice: x: 2, y: 2, z: 4, core: 2. Of those that a mesh axis runs over, the one named last changes fastest.
Arguments:
- queries: bfloat16 [2, 512, 8192], P(None, 'groups'), parts along dimension 1, may hold values from -14 to 14
- kv_cache: bfloat16 [256, 128, 2, 1024], P(('groups', 'pages')), parts along dimension 0, may hold values from -14 to 14
- w_out: bfloat16 [8192, 8192], P('pages'), may hold values from -0.0625 to 0.0625
- slot_page_before: int32 [256], P(('groups', 'pages')), parts along dimension 0, may hold values from -1 to 127, as said below
- slot_page_after: int32 [256], P(('groups', 'pages')), parts along dimension 0, may hold values from -1 to 127, as said below
- move_out: int32 [32, 4], P(('groups', 'pages')), parts along dimension 0, may hold values from -1 to 7, as said below
- move_in: int32 [32, 4], P(('groups', 'pages')), parts along dimension 0, may hold values from -1 to 7, as said below
- positions: int32 [2, 512], P(None, 'groups'), parts along dimension 1, may hold values from 0 to 16383, as said below
Outputs:
- attn_output: bfloat16 [2, 512, 8192], P(None, ('groups', 'pages')), parts along dimension 1
- cache_after: bfloat16 [256, 128, 2, 1024], P(('groups', 'pages')), parts along dimension 0
There are 2 independent parts, one for each index of `groups`. A program takes and returns all parts, laid end to end along the dimension named above; an argument that names none is the same for every part. Nothing has to cross between parts.
Inputs may be any that keep to these rules, and one draw needn't show every extreme that they name: `slot_page_before`: the logical page held by each slot; -1 marks a free slot; the live pages are the last ones of the sequence, numbered consecutively up to 127, each in exactly one slot; an owner's free slots are its last ones. `slot_page_after`: pages that are not sent keep their slot, each sent page sits in the slot that move_in names at its new owner, and a slot that sent its page is free. `move_out`: entry [j, o - 1] is a slot of owner j holding a live page, sent to owner (j + o) mod 16, or -1; the slots of one row differ; an owner sends at most one page to each of its next 4 owners. `move_in`: entry [j, o - 1] is a slot of owner j that is free before the moves, or -1, which it is exactly where move_out[(j - o) mod 16, o - 1] is -1; the slots of one row differ. Each row holds 256 consecutive positions; row 1 ends at the last position of the last live page; at most 256 positions lie between the end of row 0 and the start of row 1; all lie within the live pages.
All inputs are finite; a program needn't handle non-finite values.
Results may differ from a plain program's by a relative error of at most 0.0055.
Values may be sent and summed in bfloat16 or wider, within the bound.
No kernel may reach another device: no remote copies, remote signals or barrier semaphores. Data moves between devices by JAX's collectives and lax.ppermute only.
A program may use at most 192 MiB of HBM per device.

v0:
```python
import jax
import jax.numpy as jnp
from jax import lax
from jax.sharding import PartitionSpec as P

HEADS = 64
KV_HEADS = 8
HEAD_DIM = 128
D = 8192
PAGE_TOK = 128
BLOCK = 256
MOVE_WIN = 4


floor_score = -1e30


def passed_along(block, axis, distance):
    devices = range(lax.axis_size(axis))
    route = [((i - distance) % len(devices), i) for i in devices]
    return lax.ppermute(block, axis, route)


def block_partials(query_rows, cache_rows, slot_table, positions_row):
    key_count = cache_rows.shape[0] * PAGE_TOK
    head_group = HEADS // KV_HEADS
    key_rows = cache_rows[:, :, 0, :].reshape(key_count, KV_HEADS, HEAD_DIM)
    value_rows = cache_rows[:, :, 1, :].reshape(key_count, KV_HEADS, HEAD_DIM)
    key_pos = (
        slot_table[:, None] * PAGE_TOK + jnp.arange(PAGE_TOK, dtype=jnp.int32)[None, :]
    ).reshape(key_count)
    live_keys = jnp.repeat(slot_table >= 0, PAGE_TOK)
    sub_rows = min(64, BLOCK)
    score_scale = HEAD_DIM ** (-0.5)
    queries_in = query_rows.reshape(BLOCK // sub_rows, sub_rows, KV_HEADS, head_group, HEAD_DIM)
    places = positions_row.reshape(BLOCK // sub_rows, sub_rows)

    def one_block(inputs):
        query_block, query_pos = inputs
        scores = (
            jnp.einsum("qhgd,khd->qhgk", query_block, key_rows, preferred_element_type=jnp.float32)
            * score_scale
        )
        visible = (live_keys[None, :] & (key_pos[None, :] <= query_pos[:, None]))[:, None, None, :]
        scores = jnp.where(visible, scores, floor_score)
        row_max = jnp.max(scores, axis=-1)
        weights = jnp.where(visible, jnp.exp(scores - row_max[..., None]), 0.0).astype(jnp.bfloat16)
        row_sum = jnp.sum(weights, axis=-1, dtype=jnp.float32)
        mixed_rows = jnp.einsum(
            "qhgk,khd->qhgd", weights, value_rows, preferred_element_type=jnp.float32
        )
        return (
            mixed_rows.reshape(sub_rows, HEADS * HEAD_DIM),
            row_max.reshape(sub_rows, HEADS),
            row_sum.reshape(sub_rows, HEADS),
        )

    mixed_rows, row_max, row_sum = lax.map(one_block, (queries_in, places))
    return (
        mixed_rows.reshape(BLOCK, HEADS * HEAD_DIM),
        row_max.reshape(BLOCK, HEADS),
        row_sum.reshape(BLOCK, HEADS),
    )


def combine_parts(part_out, part_max, part_sum):
    sources, item_count, head_count = part_max.shape
    part_out = part_out.reshape(sources, item_count, head_count, HEAD_DIM)
    overall = jnp.max(part_max, axis=0)
    factor = jnp.exp(part_max - overall[None])
    weighted = jnp.sum(factor[..., None] * part_out, axis=0)
    normalizer = jnp.sum(factor * part_sum, axis=0)
    return (
        (weighted / normalizer[..., None])
        .reshape(item_count, head_count * HEAD_DIM)
        .astype(jnp.bfloat16)
    )


def migrate_pages(kv_cache, slot_page_after, move_out, move_in):
    slot_ids = jnp.arange(kv_cache.shape[0], dtype=jnp.int32)
    arranged = jnp.where(
        (slot_page_after >= 0)[:, None, None, None], kv_cache, jnp.zeros((), kv_cache.dtype)
    )
    outgoing = kv_cache[jnp.maximum(move_out[0], 0)]
    for offset in range(1, MOVE_WIN + 1):
        arrived = passed_along(outgoing[offset - 1], "pages", offset)
        landing = (slot_ids == move_in[0, offset - 1])[:, None, None, None]
        arranged = jnp.where(landing, arrived[None], arranged)
    return arranged


def local(
    queries, kv_cache, w_out, slot_page_before, slot_page_after, move_out, move_in, positions
):
    owners = lax.axis_size("pages")
    tok_rows = BLOCK // owners
    cache_after = migrate_pages(kv_cache, slot_page_after, move_out, move_in)
    results = []
    for block_index, (cache_rows, slot_table) in enumerate(
        ((kv_cache, slot_page_before), (cache_after, slot_page_after))
    ):
        part_out, part_max, part_sum = block_partials(
            queries[block_index], cache_rows, slot_table, positions[block_index]
        )
        merged = combine_parts(
            lax.all_to_all(
                part_out.reshape(1, owners, tok_rows, D),
                "pages",
                split_axis=1,
                concat_axis=0,
                tiled=True,
            )[:, 0],
            lax.all_to_all(
                part_max.reshape(1, owners, tok_rows, HEADS),
                "pages",
                split_axis=1,
                concat_axis=0,
                tiled=True,
            )[:, 0],
            lax.all_to_all(
                part_sum.reshape(1, owners, tok_rows, HEADS),
                "pages",
                split_axis=1,
                concat_axis=0,
                tiled=True,
            )[:, 0],
        )
        attended = lax.all_to_all(merged, "pages", split_axis=1, concat_axis=0, tiled=True)
        results.append(
            lax.psum_scatter(
                jnp.dot(attended, w_out, preferred_element_type=jnp.float32),
                "pages",
                scatter_dimension=0,
                tiled=True,
            ).astype(jnp.bfloat16)
        )
    return (jnp.stack(results), cache_after)


def solution(mesh):
    in_specs = (
        P(None, "groups", None),
        P(("groups", "pages"), None, None, None),
        P("pages", None),
        P(("groups", "pages")),
        P(("groups", "pages")),
        P(("groups", "pages"), None),
        P(("groups", "pages"), None),
        P(None, "groups"),
    )
    out_specs = (P(None, ("groups", "pages"), None), P(("groups", "pages"), None, None, None))
    return jax.shard_map(local, mesh=mesh, in_specs=in_specs, out_specs=out_specs, check_vma=False)
```

profile of v0, /device:TPU:0, one launch (start us, length us, event | category | flops | bytes accessed | tf_op | source)
XLA Modules:
  0.0 817.2 jit_solution(12786084088419435648)
XLA Ops:
  7.8 7.1 gather_fusion
  23.2 18.6 %slice_reduce_fusion.2 = (bf16[8,128,1024]{2,1,0:T(8,128)(2,1)S(1)}, bf16[8,128,1024]{2,1,0:T(8,128)(2,1)}) fusion(bf16[8,128,2,1024]{3,2,1,0:T(2,128)(2,1)S(1)} %copy-done.2), kind=kLoop, calls=%fused_computation.59 | loop fusion | bytes 8388608 | tf_op jit(solution)/shard_map/slice | solution.py:28
  59.0 126.6 %while.30 = (s32[]{:T(128)}, f32[4,64,8192]{2,1,0:T(8,128)}, f32[4,64,64]{2,1,0:T(8,128)S(1)}, f32[4,64,64]{2,1,0:T(8,128)S(1)}, s32[4,64]{1,0:T(4,128)S(1)}, /*...) while((s32[]{:T(128)}, f32[4,64,8192]{2,1,0:T(8,128)}, ...), condition=%wide.region_3.4_spmd.clone, body=%wide.region_0.3_spmd.clone.sunk | while | flops 2210522112 | bytes 137965520 | solution.py:58
  77.0 8.9 %fusion.58 = f32[64,8,8,128]{3,2,0,1:T(8,128)S(1)} fusion(bf16[1024,8,128]{2,0,1:T(8,128)(2,1)} %get-tuple-element.508, f32[8,64,8,1024]{3,2,1,0:T(8,128)} %copy-done, f32[64,8,8]{2,0,1:T(8,128)S(1)} %get-tuple-element.429, pred[64,1024]{1,0:T(8,128)(4,1)S(1)} %compare_and_fusion.4), kind=kOutput, calls=%fused_computation.16.clone.1 | convolution fusion | flops 1094713344 | bytes 21053440 | tf_op jit(solution)/shard_map/while/body/eval_jaxpr/qhgk,khd->qhgd/dot_general | solution.py:49
  108.6 8.9 %fusion.58 = f32[64,8,8,128]{3,2,0,1:T(8,128)S(1)} fusion(bf16[1024,8,128]{2,0,1:T(8,128)(2,1)} %get-tuple-element.508, f32[8,64,8,1024]{3,2,1,0:T(8,128)} %copy-done, f32[64,8,8]{2,0,1:T(8,128)S(1)} %get-tuple-element.429, pred[64,1024]{1,0:T(8,128)(4,1)S(1)} %compare_and_fusion.4), kind=kOutput, calls=%fused_computation.16.clone.1 | convolution fusion | flops 1094713344 | bytes 21053440 | tf_op jit(solution)/shard_map/while/body/eval_jaxpr/qhgk,khd->qhgd/dot_general | solution.py:49
  140.2 8.9 %fusion.58 = f32[64,8,8,128]{3,2,0,1:T(8,128)S(1)} fusion(bf16[1024,8,128]{2,0,1:T(8,128)(2,1)} %get-tuple-element.508, f32[8,64,8,1024]{3,2,1,0:T(8,128)} %copy-done, f32[64,8,8]{2,0,1:T(8,128)S(1)} %get-tuple-element.429, pred[64,1024]{1,0:T(8,128)(4,1)S(1)} %compare_and_fusion.4), kind=kOutput, calls=%fused_computation.16.clone.1 | convolution fusion | flops 1094713344 | bytes 21053440 | tf_op jit(solution)/shard_map/while/body/eval_jaxpr/qhgk,khd->qhgd/dot_general | solution.py:49
  171.8 8.9 %fusion.58 = f32[64,8,8,128]{3,2,0,1:T(8,128)S(1)} fusion(bf16[1024,8,128]{2,0,1:T(8,128)(2,1)} %get-tuple-element.508, f32[8,64,8,1024]{3,2,1,0:T(8,128)} %copy-done, f32[64,8,8]{2,0,1:T(8,128)S(1)} %get-tuple-element.429, pred[64,1024]{1,0:T(8,128)(4,1)S(1)} %compare_and_fusion.4), kind=kOutput, calls=%fused_computation.16.clone.1 | convolution fusion | flops 1094713344 | bytes 21053440 | tf_op jit(solution)/shard_map/while/body/eval_jaxpr/qhgk,khd->qhgd/dot_general | solution.py:49
  223.0 9.4 %mul.54 = f32[1,16,16,8192]{3,2,0,1:T(8,128)} reshape(f32[16,16,64,128]{3,2,1,0:T(8,128)} %mul.53) | data formatting | bytes 16777216 | tf_op jit(solution)/shard_map/mul | solution.py:71
  232.7 9.4 %broadcast_select_fusion.4 = bf16[8,128,2,1024]{3,2,1,0:T(2,128)(2,1)S(1)} fusion(pred[8]{0:T(512)(128)(4,1)S(1)} %get-tuple-element.307, pred[8]{0:T(512)(128)(4,1)S(1)} %get-tuple-element.306, pred[8]{0:T(512)(128)(4,1)S(1)} %get-tuple-element.305, pred[8]{0:T(512)(128)(4,1)S(1)} %get-tuple-element.304, bf16[8,128,2,1024]{3,2,1,0:T(2,128)(2,1)} %param.13, ...), kind=kLoop, calls=%fused_computation.55 | loop fusion | flops 10485760 | bytes 10485800 | tf_op jit(solution)/shard_map/jit(_where)/select_n | solution.py:89
  242.2 18.6 %slice_reduce_fusion = (bf16[8,128,1024]{2,1,0:T(8,128)(2,1)S(1)}, bf16[8,128,1024]{2,1,0:T(8,128)(2,1)}) fusion(bf16[8,128,2,1024]{3,2,1,0:T(2,128)(2,1)S(1)} %broadcast_select_fusion.4), kind=kLoop, calls=%fused_computation.56 | loop fusion | bytes 8388608 | tf_op jit(solution)/shard_map/slice | solution.py:28
  271.1 126.6 %while.31 = (s32[]{:T(128)}, f32[4,64,8192]{2,1,0:T(8,128)}, f32[4,64,64]{2,1,0:T(8,128)S(1)}, f32[4,64,64]{2,1,0:T(8,128)S(1)}, s32[4,64]{1,0:T(4,128)S(1)}, /*...) while((s32[]{:T(128)}, f32[4,64,8192]{2,1,0:T(8,128)}, ...), condition=%wide.region_11.12_spmd.clone, body=%wide.region_8.11_spmd.clone.sunk | while | flops 2210522112 | bytes 137965520 | solution.py:58
  289.2 8.9 %fusion.62 = f32[64,8,8,128]{3,2,0,1:T(8,128)S(1)} fusion(bf16[1024,8,128]{2,0,1:T(8,128)(2,1)} %get-tuple-element.475, f32[8,64,8,1024]{3,2,1,0:T(8,128)} %copy-done.1, f32[64,8,8]{2,0,1:T(8,128)S(1)} %get-tuple-element.443, pred[64,1024]{1,0:T(8,128)(4,1)S(1)} %compare_and_fusion.5), kind=kOutput, calls=%fused_computation.38.clone.1 | convolution fusion | flops 1094713344 | bytes 21053440 | tf_op jit(solution)/shard_map/while/body/eval_jaxpr/qhgk,khd->qhgd/dot_general | solution.py:49
  320.7 8.9 %fusion.62 = f32[64,8,8,128]{3,2,0,1:T(8,128)S(1)} fusion(bf16[1024,8,128]{2,0,1:T(8,128)(2,1)} %get-tuple-element.475, f32[8,64,8,1024]{3,2,1,0:T(8,128)} %copy-done.1, f32[64,8,8]{2,0,1:T(8,128)S(1)} %get-tuple-element.443, pred[64,1024]{1,0:T(8,128)(4,1)S(1)} %compare_and_fusion.5), kind=kOutput, calls=%fused_computation.38.clone.1 | convolution fusion | flops 1094713344 | bytes 21053440 | tf_op jit(solution)/shard_map/while/body/eval_jaxpr/qhgk,khd->qhgd/dot_general | solution.py:49
  352.4 8.9 %fusion.62 = f32[64,8,8,128]{3,2,0,1:T(8,128)S(1)} fusion(bf16[1024,8,128]{2,0,1:T(8,128)(2,1)} %get-tuple-element.475, f32[8,64,8,1024]{3,2,1,0:T(8,128)} %copy-done.1, f32[64,8,8]{2,0,1:T(8,128)S(1)} %get-tuple-element.443, pred[64,1024]{1,0:T(8,128)(4,1)S(1)} %compare_and_fusion.5), kind=kOutput, calls=%fused_computation.38.clone.1 | convolution fusion | flops 1094713344 | bytes 21053440 | tf_op jit(solution)/shard_map/while/body/eval_jaxpr/qhgk,khd->qhgd/dot_general | solution.py:49
  384.0 8.9 %fusion.62 = f32[64,8,8,128]{3,2,0,1:T(8,128)S(1)} fusion(bf16[1024,8,128]{2,0,1:T(8,128)(2,1)} %get-tuple-element.475, f32[8,64,8,1024]{3,2,1,0:T(8,128)} %copy-done.1, f32[64,8,8]{2,0,1:T(8,128)S(1)} %get-tuple-element.443, pred[64,1024]{1,0:T(8,128)(4,1)S(1)} %compare_and_fusion.5), kind=kOutput, calls=%fused_computation.38.clone.1 | convolution fusion | flops 1094713344 | bytes 21053440 | tf_op jit(solution)/shard_map/while/body/eval_jaxpr/qhgk,khd->qhgd/dot_general | solution.py:49
  418.6 6.6 all-to-all-done.6
  425.2 12.6 %all_to_all.86 = bf16[16,16,512]{2,0,1:T(8,128)(2,1)S(1)} all-to-all(bf16[16,16,512]{2,0,1:T(8,128)(2,1)S(1)} %copy.53), channel_id=1, replica_groups=mesh['groups'=2,'pages'=16] {'pages'}, dimensions={1} | all-to-all | bytes 524288 | tf_op jit(solution)/shard_map/all_to_all | solution.py:129
  442.7 9.0 %fusion.41 = f32[256,8192]{1,0:T(8,128)} fusion(bf16[256,512]{1,0:T(8,128)(2,1)S(1)} %bitcast.262, bf16[512,8192]{1,0:T(8,128)(2,1)} %param.14), kind=kOutput, calls=%fused_computation.96 | convolution fusion | flops 2147483648 | bytes 17039360 | tf_op jit(solution)/shard_map/dot_general | solution.py:132
  458.3 9.8 %mul.59 = f32[1,16,16,8192]{3,2,0,1:T(8,128)} reshape(f32[16,16,64,128]{3,2,1,0:T(8,128)} %mul.58) | data formatting | bytes 16777216 | tf_op jit(solution)/shard_map/mul | solution.py:71
  468.3 158.6 %all-to-all-done.5 = f32[1,16,16,8192]{3,2,0,1:T(8,128)} async-done(((f32[1,16,16,8192]{3,2,0,1:T(8,128)}), f32[1,16,16,8192]{3,2,0,1:T(8,128)}, u32[]{:S(2)}, u32[]{:S(2)}) %all-to-all-start.5) | async-done | bytes 8388640 | tf_op jit(solution)/shard_map/all_to_all | solution.py:107
  626.9 7.0 multiply_reduce_fusion
  634.4 62.7 %all_to_all.87 = bf16[16,16,512]{2,0,1:T(8,128)(2,1)S(1)} all-to-all(bf16[16,16,512]{2,0,1:T(8,128)(2,1)S(1)} %copy.61), channel_id=1, replica_groups=mesh['groups'=2,'pages'=16] {'pages'}, dimensions={1} | all-to-all | bytes 524288 | tf_op jit(solution)/shard_map/all_to_all | solution.py:129
  697.1 9.0 %fusion.42 = f32[256,8192]{1,0:T(8,128)} fusion(bf16[256,512]{1,0:T(8,128)(2,1)S(1)} %bitcast.263, bf16[512,8192]{1,0:T(8,128)(2,1)} %param.14), kind=kOutput, calls=%fused_computation.97 | convolution fusion | flops 2147483648 | bytes 17039360 | tf_op jit(solution)/shard_map/dot_general | solution.py:132
  707.3 100.7 %reduce-scatter.5.cloned.1.call-done = f32[16,8192]{1,0:T(8,128)} async-done(((f32[256,8192]{1,0:T(8,128)}), f32[16,8192]{1,0:T(8,128)}) %reduce-scatter.5.cloned.1.call-update) | async-done | bytes 524304 | tf_op jit(solution)/shard_map/reduce_scatter | solution.py:131
  (228 shorter events, 290.9 us)
Async XLA Ops:
  14.9 8.3 %copy-start.2 = (bf16[8,128,2,1024]{3,2,1,0:T(2,128)(2,1)S(1)}, bf16[8,128,2,1024]{3,2,1,0:T(2,128)(2,1)}, u32[]{:S(2)}) copy-start(bf16[8,128,2,1024]{3,2,1,0:T(2,128)(2,1)} %param.13) | copy-start | bytes 12582916
  14.9 26.9 %copy-start.7 = (s32[8]{0:T(128)S(1)}, s32[8]{0:T(128)}, u32[]{:S(2)}) copy-start(s32[8]{0:T(128)} %param.15) | copy-start | bytes 100
  17.3 215.4 %collective-permute-start = (bf16[128,2,1024]{2,1,0:T(2,128)(2,1)}, bf16[128,2,1024]{2,1,0:T(2,128)(2,1)}, u32[]{:S(2)}, u32[]{:S(2)}) collective-permute-start(bf16[128,2,1024]{2,1,0:T(2,128)(2,1)} %get-tuple-element.296), channel_id=1, source_target_pairs={{12,0},{13,1},{14,2},{15,3},{0,4},{1,5},{2,6},{3,7},{4,8},{5,9},{6... | collective-permute-start | bytes 1572872 | tf_op jit(solution)/shard_map/ppermute | solution.py:21
  20.4 212.4 %collective-permute-start.1 = (bf16[128,2,1024]{2,1,0:T(2,128)(2,1)}, bf16[128,2,1024]{2,1,0:T(2,128)(2,1)}, u32[]{:S(2)}, u32[]{:S(2)}) collective-permute-start(bf16[128,2,1024]{2,1,0:T(2,128)(2,1)} %get-tuple-element.298), channel_id=1, source_target_pairs={{13,0},{14,1},{15,2},{0,3},{1,4},{2,5},{3,6},{4,7},{5,8},{6,9},{7,... | collective-permute-start | bytes 1572872 | tf_op jit(solution)/shard_map/ppermute | solution.py:21
  21.0 211.7 %collective-permute-start.2 = (bf16[128,2,1024]{2,1,0:T(2,128)(2,1)}, bf16[128,2,1024]{2,1,0:T(2,128)(2,1)}, u32[]{:S(2)}, u32[]{:S(2)}) collective-permute-start(bf16[128,2,1024]{2,1,0:T(2,128)(2,1)} %get-tuple-element.297), channel_id=1, source_target_pairs={{14,0},{15,1},{0,2},{1,3},{2,4},{3,5},{4,6},{5,7},{6,8},{7,9},{8,1... | collective-permute-start | bytes 1572872 | tf_op jit(solution)/shard_map/ppermute | solution.py:21
  22.6 210.2 %collective-permute-start.3 = (bf16[128,2,1024]{2,1,0:T(2,128)(2,1)}, bf16[128,2,1024]{2,1,0:T(2,128)(2,1)}, u32[]{:S(2)}, u32[]{:S(2)}) collective-permute-start(bf16[128,2,1024]{2,1,0:T(2,128)(2,1)} %get-tuple-element.299), channel_id=1, source_target_pairs={{15,0},{0,1},{1,2},{2,3},{3,4},{4,5},{5,6},{6,7},{7,8},{8,9},{9,10... | collective-permute-start | bytes 1572872 | tf_op jit(solution)/shard_map/ppermute | solution.py:21
  59.0 132.5 %copy-start.8 = (s32[8]{0:T(128)S(1)}, s32[8]{0:T(128)}, u32[]{:S(2)}) copy-start(s32[8]{0:T(128)} %param.16) | copy-start | bytes 100
  59.0 133.3 %copy-start.5 = (s32[1,4]{1,0:T(1,128)S(1)}, s32[1,4]{1,0:T(1,128)}, u32[]{:S(2)}) copy-start(s32[1,4]{1,0:T(1,128)} %param.18) | copy-start | bytes 52
  64.7 5.7 copy-start
  96.4 5.7 copy-start
  127.9 5.7 copy-start
  159.5 5.7 copy-start
  186.4 12.1 %all-to-all-start = ((f32[16,1,1024]{2,1,0:T(1,128)}), f32[16,1,1024]{2,1,0:T(1,128)S(1)}, u32[]{:S(2)}, u32[]{:S(2)}) async-start(f32[16,1,1024]{2,1,0:T(1,128)} %reshape.268), calls=%async_computation | async-start | bytes 131072 | tf_op jit(solution)/shard_map/all_to_all | solution.py:114
  198.4 12.9 %all-to-all-start.2 = ((f32[16,1,1024]{2,1,0:T(1,128)}), f32[16,1,1024]{2,1,0:T(1,128)S(1)}, u32[]{:S(2)}, u32[]{:S(2)}) async-start(f32[16,1,1024]{2,1,0:T(1,128)} %reshape.270), calls=%async_computation.2 | async-start | bytes 131072 | tf_op jit(solution)/shard_map/all_to_all | solution.py:121
  211.3 187.9 %all-to-all-start.1 = ((f32[1,16,16,8192]{3,2,0,1:T(8,128)}), f32[1,16,16,8192]{3,2,0,1:T(8,128)}, u32[]{:S(2)}, u32[]{:S(2)}) async-start(f32[1,16,16,8192]{3,2,0,1:T(8,128)} %bitcast.245), calls=%async_computation.1 | async-start | bytes 16777216 | tf_op jit(solution)/shard_map/all_to_all | solution.py:107
  242.2 20.8 %copy-start.3 = (bf16[8,128,2,1024]{3,2,1,0:T(2,128)(2,1)}, bf16[8,128,2,1024]{3,2,1,0:T(2,128)(2,1)S(1)}, u32[]{:S(2)}) copy-start(bf16[8,128,2,1024]{3,2,1,0:T(2,128)(2,1)S(1)} %broadcast_select_fusion.4) | copy-start | bytes 12582916
  276.9 5.7 copy-start.1
  308.5 5.7 copy-start.1
  340.1 5.7 copy-start.1
  399.3 13.0 %all-to-all-start.4 = ((f32[16,1,1024]{2,1,0:T(1,128)}), f32[16,1,1024]{2,1,0:T(1,128)S(1)}, u32[]{:S(2)}, u32[]{:S(2)}) async-start(f32[16,1,1024]{2,1,0:T(1,128)} %reshape.264), calls=%async_computation.5 | async-start | bytes 131072 | tf_op jit(solution)/shard_map/all_to_all | solution.py:114
  412.3 12.9 %all-to-all-start.6 = ((f32[16,1,1024]{2,1,0:T(1,128)}), f32[16,1,1024]{2,1,0:T(1,128)S(1)}, u32[]{:S(2)}, u32[]{:S(2)}) async-start(f32[16,1,1024]{2,1,0:T(1,128)} %reshape.266), calls=%async_computation.7 | async-start | bytes 131072 | tf_op jit(solution)/shard_map/all_to_all | solution.py:121
  437.8 189.1 %all-to-all-start.5 = ((f32[1,16,16,8192]{3,2,0,1:T(8,128)}), f32[1,16,16,8192]{3,2,0,1:T(8,128)}, u32[]{:S(2)}, u32[]{:S(2)}) async-start(f32[1,16,16,8192]{3,2,0,1:T(8,128)} %bitcast.244), calls=%async_computation.6 | async-start | bytes 16777216 | tf_op jit(solution)/shard_map/all_to_all | solution.py:107
  442.6 263.6 %reduce-scatter.3.cloned.1.call-start = ((), (), s32[]{:S(2)}) async-start(), calls=%async_computation.10 | async-start | bytes 8912896 | tf_op jit(solution)/shard_map/reduce_scatter | solution.py:131
  451.7 356.3 %reduce-scatter.5.cloned.1.call-start = ((), (), s32[]{:S(2)}) async-start(), calls=%async_computation.11 | async-start | bytes 8912896 | tf_op jit(solution)/shard_map/reduce_scatter | solution.py:131
  (3 other events, 14.0 us)
Sparse Core Ops, SparseCore 0:
  451.8 206.1 reduce-scatter.2
  706.3 101.6 reduce-scatter.4
where the time goes:
time: 826 us; the launch traced here: 817 us
  waiting for transfers between devices  271 us (33%)
  local copies, waits for them, and re-layouts  203 us (25%)
  matrix products  131 us (16%)
  other arithmetic  82.8 us (10%)
  blocking collectives  75.3 us (9%)
  starting transfers between devices  37.8 us (5%)
  between operations  15 us (2%)
    all_to_all x2, waiting for transfers between devices, local(): lax.all_to_all(part_out.reshape(1, owners, tok_rows, D), 'pages', split_a...  159 us
    reduce_scatter x2, waiting for transfers between devices, local(): lax.psum_scatter(jnp.dot(attended, w_out, preferred_element_type=jnp.floa...  101 us
    all_to_all x2, blocking collectives, local(): lax.all_to_all(merged, 'pages', split_axis=1, concat_axis=0, tiled=True)  75.3 us
    dot_general x8, matrix products, one_block(): jnp.einsum('qhgk,khd->qhgd', weights, value_rows, preferred_element_type=...  71.5 us
    reduce_sum x8, other arithmetic, one_block(): row_sum = jnp.sum(weights, axis=-1, dtype=jnp.float32)  49 us
    while x16, local copies, waits for them, and re-layouts  45.6 us
    dot_general x8, matrix products, one_block(): jnp.einsum('qhgd,khd->qhgk', query_block, key_rows, preferred_element_typ...  41.9 us
    slice x2, local copies, waits for them, and re-layouts, block_partials(): value_rows = cache_rows[:, :, 1, :].reshape(key_count, KV_HEADS, HEAD_DIM)  37.2 us
  transfers between devices with their start and end apart: 12, of which 4 were waited for; matrix products, arithmetic and copies ran while one was open for 44% of the time, Pallas kernels for 0%

commit v1 on v0

v1 whole, which is shorter than its diff:
```python
import functools

import jax
import jax.numpy as jnp
from jax import lax
from jax.experimental import pallas as pl
from jax.experimental.pallas import tpu as pltpu
from jax.sharding import PartitionSpec as P

HEADS = 64
KV_HEADS = 8
HEAD_DIM = 128
D = 8192
PAGE_TOK = 128
BLOCK = 256
MOVE_WIN = 4
GROUP = HEADS // KV_HEADS

LOG2E = 1.4426950408889634
FLOOR = -1e30
FAR = 1 << 30


def bits_of(n):
    return n.bit_length() - 1


def permute_to(x, n, target):
    return lax.ppermute(x, "pages", [(i, target(i)) for i in range(n)])


def head_of(j):
    half = KV_HEADS // 2
    return (j % 2) * half + j // 2


def attend_kernel(
    order, counts, x_ref, q_ref, qpos_ref, kpos_ref, *refs, first, last, tile, rows, tok
):
    n_in = 0 if first else 2
    carried = refs[:n_in]
    outs = refs[n_in : n_in + 2]
    k_s, v_s, acc_s, m_s = refs[n_in + 2 :]
    step = pl.program_id(0)
    per_tile = tile // PAGE_TOK
    n_full = counts[0]
    n_tiles = counts[1]
    src_slots = x_ref.shape[1]

    @pl.when(step == 0)
    def _():
        row = lax.broadcasted_iota(jnp.int32, (2 * PAGE_TOK, 2 * PAGE_TOK), 0)
        col = lax.broadcasted_iota(jnp.int32, (2 * PAGE_TOK, 2 * PAGE_TOK), 1)
        want = jnp.where(row < PAGE_TOK, 2 * row, 2 * (row - PAGE_TOK) + 1)
        pick = jnp.where(col == want, 1.0, 0.0).astype(jnp.bfloat16)
        ones = jnp.ones((PAGE_TOK, HEAD_DIM), jnp.bfloat16)

        def split_tile(i, carry):
            for s in range(per_tile):
                slot = order[i * per_tile + s]
                both = jnp.dot(
                    pick,
                    x_ref[slot // src_slots, slot % src_slots],
                    preferred_element_type=jnp.float32,
                ).astype(jnp.bfloat16)
                at = pl.multiple_of(i * tile + s * PAGE_TOK, PAGE_TOK)
                k_s[pl.ds(at, PAGE_TOK), :] = both[:PAGE_TOK]
                v_s[pl.ds(at, PAGE_TOK), :HEAD_DIM] = both[PAGE_TOK:]
                v_s[pl.ds(at, PAGE_TOK), HEAD_DIM:] = ones
            return carry

        lax.fori_loop(0, n_tiles, split_tile, 0)

    total = GROUP * tok
    if first:
        m_s[...] = jnp.full(m_s.shape, FLOOR, jnp.float32)
        acc_s[...] = jnp.zeros(acc_s.shape, jnp.float32)
    else:
        acc_s[...] = carried[0][0]
        m_s[...] = carried[1][0]

    scale = HEAD_DIM**-0.5 * LOG2E

    def tile_step(i, carry, masked):
        at = pl.multiple_of(i * tile, tile)
        keys = k_s[pl.ds(at, tile), :]
        values = v_s[pl.ds(at, tile), :]
        if masked:
            visible = kpos_ref[pl.ds(i, 1), :] <= qpos_ref[0]
            visible = jnp.concatenate([visible] * (rows // tok), axis=0)
        for part in range(total // rows):
            span = slice(part * rows, (part + 1) * rows)
            scores = lax.dot_general(
                q_ref[0, span, :],
                keys,
                (((1,), (1,)), ((), ())),
                preferred_element_type=jnp.float32,
            )
            if masked:
                scores = jnp.where(visible, scores, FLOOR)
            m_old = m_s[span, :]
            m_new = jnp.maximum(m_old, jnp.max(scores, axis=1, keepdims=True) * scale)
            shift = jnp.maximum(m_new, 0.5 * FLOOR * scale)[:, :1]
            weights = jnp.exp2(scores * scale - shift).astype(jnp.bfloat16)
            alpha = jnp.exp2(m_old - m_new)
            mixed = jnp.dot(weights, values, preferred_element_type=jnp.float32)
            acc_s[span, :HEAD_DIM] = acc_s[span, :HEAD_DIM] * alpha + mixed[:, :HEAD_DIM]
            acc_s[span, HEAD_DIM:] = acc_s[span, HEAD_DIM:] * alpha + mixed[:, HEAD_DIM:]
            m_s[span, :] = m_new
        return carry

    lax.fori_loop(0, n_full, functools.partial(tile_step, masked=False), 0)
    lax.fori_loop(n_full, n_tiles, functools.partial(tile_step, masked=True), 0)

    if not last:
        outs[0][0] = acc_s[...]
        outs[1][0] = m_s[...]
    else:
        out_ref, ml_ref = outs
        out_ref[0] = acc_s[:, :HEAD_DIM].astype(jnp.bfloat16)
        row = lax.broadcasted_iota(jnp.int32, (tok, HEAD_DIM), 0)
        col = lax.broadcasted_iota(jnp.int32, (tok, HEAD_DIM), 1)
        eye = row == col
        for g in range(GROUP):
            span = slice(g * tok, (g + 1) * tok)
            ml_ref[0, 0, g : g + 1, :] = jnp.sum(
                jnp.where(eye, m_s[span, :], 0.0), axis=0, keepdims=True
            )
            ml_ref[0, 1, g : g + 1, :] = jnp.sum(
                jnp.where(eye, acc_s[span, HEAD_DIM:], 0.0), axis=0, keepdims=True
            )


def attend(x, q, qpos, kpos, order, counts, carried, last, tile, rows):
    sources, src_slots = x.shape[:2]
    steps, total, _ = q.shape
    tok = total // GROUP
    first = carried is None
    n_slots = sources * src_slots
    spec3 = lambda i, *_: (i, 0, 0)
    spec4 = lambda i, *_: (i, 0, 0, 0)
    fixed2 = lambda i, *_: (0, 0)
    in_specs = [
        pl.BlockSpec(x.shape, lambda i, *_: (0, 0, 0, 0)),
        pl.BlockSpec((1, total, HEAD_DIM), spec3),
        pl.BlockSpec((1, tok, 1), spec3),
        pl.BlockSpec(kpos.shape, fixed2),
    ]
    if last:
        out_shape = (
            jax.ShapeDtypeStruct((steps, total, HEAD_DIM), jnp.bfloat16),
            jax.ShapeDtypeStruct((steps, 2, GROUP, HEAD_DIM), jnp.float32),
        )
        out_specs = (
            pl.BlockSpec((1, total, HEAD_DIM), spec3),
            pl.BlockSpec((1, 2, GROUP, HEAD_DIM), spec4),
        )
    else:
        out_shape = (
            jax.ShapeDtypeStruct((steps, total, 2 * HEAD_DIM), jnp.float32),
            jax.ShapeDtypeStruct((steps, total, HEAD_DIM), jnp.float32),
        )
        out_specs = (
            pl.BlockSpec((1, total, 2 * HEAD_DIM), spec3),
            pl.BlockSpec((1, total, HEAD_DIM), spec3),
        )
    extra = ()
    if not first:
        extra = tuple(carried)
        in_specs += [
            pl.BlockSpec((1, total, 2 * HEAD_DIM), spec3),
            pl.BlockSpec((1, total, HEAD_DIM), spec3),
        ]
    flops = 4 * steps * total * n_slots * PAGE_TOK * HEAD_DIM
    return pl.pallas_call(
        functools.partial(
            attend_kernel, first=first, last=last, tile=tile, rows=rows, tok=tok
        ),
        out_shape=out_shape,
        grid_spec=pltpu.PrefetchScalarGridSpec(
            num_scalar_prefetch=2,
            grid=(steps,),
            in_specs=in_specs,
            out_specs=out_specs,
            scratch_shapes=[
                pltpu.VMEM((n_slots * PAGE_TOK, HEAD_DIM), jnp.bfloat16),
                pltpu.VMEM((n_slots * PAGE_TOK, 2 * HEAD_DIM), jnp.bfloat16),
                pltpu.VMEM((total, 2 * HEAD_DIM), jnp.float32),
                pltpu.VMEM((total, HEAD_DIM), jnp.float32),
            ],
        ),
        cost_estimate=pl.CostEstimate(
            flops=flops,
            transcendentals=flops // (4 * HEAD_DIM),
            bytes_accessed=x.size * 2 + q.size * 2,
        ),
        name="attend_last" if last else "attend_first",
    )(order, counts, x, q, qpos, kpos, *extra)


def project_kernel(*refs, parts, tok):
    outs = refs[:parts]
    mls = refs[parts : 2 * parts]
    ws = refs[2 * parts : 3 * parts]
    keep_ref, send_ref, a_s = refs[3 * parts :]

    @pl.when(pl.program_id(0) == 0)
    def _():
        row = lax.broadcasted_iota(jnp.int32, (tok, HEAD_DIM), 0)
        col = lax.broadcasted_iota(jnp.int32, (tok, HEAD_DIM), 1)
        eye = row == col
        for g in range(GROUP):
            ms = [ml[0, g : g + 1, :] for ml in mls]
            top = functools.reduce(jnp.maximum, ms)
            factors = [jnp.exp2(m - top) for m in ms]
            total = sum(f * ml[1, g : g + 1, :] for f, ml in zip(factors, mls))
            span = slice(g * tok, (g + 1) * tok)
            mixed = 0.0
            for f, out in zip(factors, outs):
                ratio = jnp.where(eye, f / total, 0.0)
                mixed += jnp.sum(ratio, axis=1, keepdims=True) * out[span, :].astype(
                    jnp.float32
                )
            a_s[:, g * HEAD_DIM : (g + 1) * HEAD_DIM] = mixed.astype(jnp.bfloat16)

    depth = a_s.shape[1] // parts
    total = 0.0
    for s in range(parts):
        total += jnp.dot(
            a_s[:, s * depth : (s + 1) * depth], ws[s][...], preferred_element_type=jnp.float32
        )
    half = tok // 2
    keep_ref[...] = total[:half]
    send_ref[...] = total[half:].astype(jnp.bfloat16)


def project(outs, mls, ws, tok, width):
    parts = len(outs)
    columns = ws[0].shape[1]
    fixed2 = lambda i: (0, 0)
    fixed3 = lambda i: (0, 0, 0)
    half = tok // 2
    depth = sum(w.shape[0] for w in ws)
    return pl.pallas_call(
        functools.partial(project_kernel, parts=parts, tok=tok),
        out_shape=(
            jax.ShapeDtypeStruct((half, columns), jnp.float32),
            jax.ShapeDtypeStruct((half, columns), jnp.bfloat16),
        ),
        grid=(columns // width,),
        in_specs=[pl.BlockSpec(o.shape, fixed2) for o in outs]
        + [pl.BlockSpec(m.shape, fixed3) for m in mls]
        + [pl.BlockSpec((w.shape[0], width), lambda i: (0, i)) for w in ws],
        out_specs=(
            pl.BlockSpec((half, width), lambda i: (0, i)),
            pl.BlockSpec((half, width), lambda i: (0, i)),
        ),
        scratch_shapes=[pltpu.VMEM((tok, depth), jnp.bfloat16)],
        cost_estimate=pl.CostEstimate(
            flops=2 * tok * depth * columns, transcendentals=0, bytes_accessed=2 * depth * columns
        ),
        name="project",
    )(*outs, *mls, *ws)


def migrate_pages(kv_cache, outgoing, slot_page_after, move_in, n):
    slot_ids = jnp.arange(kv_cache.shape[0], dtype=jnp.int32)
    arranged = jnp.where(
        (slot_page_after >= 0)[:, None, None, None], kv_cache, jnp.zeros((), kv_cache.dtype)
    )
    for offset in range(1, MOVE_WIN + 1):
        arrived = permute_to(outgoing[offset - 1], n, lambda i: (i + offset) % n)
        landing = (slot_ids == move_in[0, offset - 1])[:, None, None, None]
        arranged = jnp.where(landing, arrived[None], arranged)
    return arranged


def local(
    queries, kv_cache, w_out, slot_page_before, slot_page_after, move_out, move_in, positions
):
    n = lax.axis_size("pages")
    slots = kv_cache.shape[0]
    ways = n // KV_HEADS
    tok_rows = BLOCK // n
    tok = BLOCK // ways
    gp = GROUP // ways
    me = lax.axis_index("pages")
    u = me // KV_HEADS
    j = me % KV_HEADS
    head = head_of(j)
    groups = [[a * KV_HEADS + b for b in range(KV_HEADS)] for a in range(ways)]
    dest_head = [head_of(b) for b in range(KV_HEADS)]

    chunks = 2
    per = slots // chunks
    by_head = kv_cache.reshape(slots, PAGE_TOK, 2, KV_HEADS, HEAD_DIM)
    by_head = jnp.transpose(by_head, (3, 0, 1, 2, 4))
    by_dest = jnp.concatenate([by_head[h : h + 1] for h in dest_head], axis=0)
    arrived = []
    for c in range(chunks):
        piece = by_dest[:, c * per : (c + 1) * per]
        got = lax.all_to_all(
            piece, "pages", 0, 0, axis_index_groups=groups, tiled=True
        )
        arrived.append(got.reshape(KV_HEADS, per, 2 * PAGE_TOK, HEAD_DIM))
    table = lax.all_to_all(
        jnp.broadcast_to(slot_page_before[None, None], (KV_HEADS, 1, slots)),
        "pages",
        0,
        0,
        axis_index_groups=groups,
        tiled=True,
    ).reshape(KV_HEADS, slots)

    xs = lambda m: jnp.arange(m, dtype=jnp.int32)
    t_of = u ^ xs(ways)
    kx = (xs(KV_HEADS) % (KV_HEADS // 2)) * 2 + xs(KV_HEADS) // (KV_HEADS // 2)
    owner = (kx[None, :] ^ head) * ways + t_of[:, None]
    g_of = ((xs(GROUP) // gp)[None, :] ^ t_of[:, None]) * gp + (xs(GROUP) % gp)[None, :]
    mine = lax.dynamic_slice_in_dim(queries, head * GROUP * HEAD_DIM, GROUP * HEAD_DIM, axis=2)
    mine = mine.reshape(2, n, tok_rows, GROUP, HEAD_DIM)
    pos = positions.reshape(2, n, tok_rows)
    q_rows = []
    q_pos = []
    for tx in range(ways):
        taken = jnp.take(jnp.take(mine, owner[tx], axis=1), g_of[tx], axis=3)
        q_rows.append(jnp.transpose(taken, (0, 3, 1, 2, 4)).reshape(2, GROUP * tok, HEAD_DIM))
        q_pos.append(jnp.take(pos, owner[tx], axis=1).reshape(2, tok, 1))
    q = jnp.concatenate(q_rows, axis=0)
    qpos = jnp.concatenate(q_pos, axis=0)

    tile = 1024
    rows = 2 * tok
    lowest = jnp.min(positions)
    carried = None
    for c in range(chunks):
        pages = table[:, c * per : (c + 1) * per].reshape(-1)
        live = pages >= 0
        full = live & (pages * PAGE_TOK + (PAGE_TOK - 1) <= lowest)
        rank = jnp.where(full, 0, jnp.where(live, 1, 2))
        order = jnp.argsort(rank, stable=True).astype(jnp.int32)
        n_live = jnp.sum(live.astype(jnp.int32)) * PAGE_TOK
        n_full = jnp.sum(full.astype(jnp.int32)) * PAGE_TOK
        counts = jnp.stack([n_full // tile, (n_live + tile - 1) // tile]).astype(jnp.int32)
        start = jnp.where(live, pages * PAGE_TOK, FAR)[order]
        kpos = (start[:, None] + xs(PAGE_TOK)[None, :]).reshape(-1, tile)
        carried = attend(
            arrived[c], q, qpos, kpos, order, counts, carried, c == chunks - 1, tile, rows
        )
    out, ml = carried
    out = out.reshape(ways, 2, GROUP * tok, HEAD_DIM)
    ml = ml.reshape(ways, 2, 2, GROUP, HEAD_DIM)

    ws = [w_out] + [permute_to(w_out, n, lambda i: i ^ s) for s in range(1, ways)]

    def merger(i, s):
        return head_of(i % KV_HEADS) * ways + ((i // KV_HEADS) ^ s)

    results = []
    for b in range(2):
        got_out = [permute_to(out[s, b], n, lambda i: merger(i, s)) for s in range(ways)]
        got_ml = [permute_to(ml[s, b], n, lambda i: merger(i, s)) for s in range(ways)]
        keep, send = project(got_out, got_ml, ws, tok, 1024)
        got = permute_to(send, n, lambda i: i ^ ways)
        total = (keep + got.astype(jnp.float32)).reshape(KV_HEADS // 2, tok_rows, D)
        mine_rows = total[0]
        for zx in range(1, KV_HEADS // 2):
            got = permute_to(
                total[zx].astype(jnp.bfloat16), n, lambda i: i ^ (zx * 2 * ways)
            )
            mine_rows = mine_rows + got.astype(jnp.float32)
        results.append(mine_rows.astype(jnp.bfloat16))

    outgoing = kv_cache[jnp.maximum(move_out[0], 0)]
    cache_after = migrate_pages(kv_cache, outgoing, slot_page_after, move_in, n)
    return (jnp.stack(results), cache_after)


def solution(mesh):
    in_specs = (
        P(None, "groups", None),
        P(("groups", "pages"), None, None, None),
        P("pages", None),
        P(("groups", "pages")),
        P(("groups", "pages")),
        P(("groups", "pages"), None),
        P(("groups", "pages"), None),
        P(None, "groups"),
    )
    out_specs = (P(None, ("groups", "pages"), None), P(("groups", "pages"), None, None, None))
    return jax.shard_map(local, mesh=mesh, in_specs=in_specs, out_specs=out_specs, check_vma=False)
```

time: 826 us -> 282 us (0.34)
  waiting for transfers between devices: 271 us -> 88.5 us
  local copies, waits for them, and re-layouts: 203 us -> 39.3 us
  matrix products: 131 us -> 0 us
  Pallas kernels: 0 us -> 81.7 us
  blocking collectives: 75.3 us -> 0 us
  other arithmetic: 82.8 us -> 23.9 us
  between operations: 15 us -> 3.77 us
    all_to_all x6 -> x3, waiting for transfers between devices: 171 us -> 18.3 us  [the longest x2 18.3 us: local(): lax.all_to_all(piece, 'pages', 0, 0, axis_index_groups=groups, tiled=True)]
    dot_general x18 -> x0, matrix products: 131 us -> none  [the longest x8 71.5 us: one_block(): jnp.einsum('qhgk,khd->qhgd', weights, value_rows, preferred_element_type=...]
    reduce_scatter x2 -> x0, waiting for transfers between devices: 101 us -> none  [local(): lax.psum_scatter(jnp.dot(attended, w_out, preferred_element_type=jnp.floa...]
    pallas_call x0 -> x4, Pallas kernels: none -> 81.7 us  [the longest x2 59.9 us: attend(): pl.pallas_call(functools.partial(attend_kernel, first=first, last=last, t...]
    all_to_all x2 -> x0, blocking collectives: 75.3 us -> none  [local(): lax.all_to_all(merged, 'pages', split_axis=1, concat_axis=0, tiled=True)]
    ppermute x4 -> x21, waiting for transfers between devices: 0.01 us -> 70.2 us  [permute_to(): return lax.ppermute(x, 'pages', [(i, target(i)) for i in range(n)])]
    reduce_sum x12 -> x1, other arithmetic: 62.6 us -> 1.46 us  [local(): n_full = jnp.sum(full.astype(jnp.int32)) * PAGE_TOK]
    while x16 -> x0, local copies, waits for them, and re-layouts: 45.6 us -> none
  transfers between devices with their start and end apart: 12 -> 24, of which waited for: 4 -> 8; matrix products, arithmetic and copies ran while one was open for 44% -> 21% of each run, Pallas kernels for 0% -> 29%
where the time goes in v1:
time: 282 us; the launch traced here: 277 us
  waiting for transfers between devices  88.5 us (31%)
  Pallas kernels  81.7 us (29%)
  starting transfers between devices  40 us (14%)
  local copies, waits for them, and re-layouts  39.3 us (14%)
  other arithmetic  23.9 us (8%)
  between operations  3.77 us (1%)
    ppermute x21, waiting for transfers between devices, permute_to(): return lax.ppermute(x, 'pages', [(i, target(i)) for i in range(n)])  70.2 us
    pallas_call x2, Pallas kernels, attend(): pl.pallas_call(functools.partial(attend_kernel, first=first, last=last, t...  59.9 us
    ppermute x21, starting transfers between devices, permute_to(): return lax.ppermute(x, 'pages', [(i, target(i)) for i in range(n)])  25.7 us
    pallas_call x2, Pallas kernels, project(): pl.pallas_call(functools.partial(project_kernel, parts=parts, tok=tok), o...  21.8 us
    all_to_all x2, waiting for transfers between devices, local(): lax.all_to_all(piece, 'pages', 0, 0, axis_index_groups=groups, tiled=True)  18.3 us
    select_n x1, other arithmetic, migrate_pages(): arranged = jnp.where(landing, arrived[None], arranged)  10.1 us
    all_to_all x2, starting transfers between devices, local(): lax.all_to_all(piece, 'pages', 0, 0, axis_index_groups=groups, tiled=True)  9.05 us
    gather x1, local copies, waits for them, and re-layouts, local(): outgoing = kv_cache[jnp.maximum(move_out[0], 0)]  7.04 us
  transfers between devices with their start and end apart: 24, of which 8 were waited for; matrix products, arithmetic and copies ran while one was open for 21% of the time, Pallas kernels for 29%

profile of v1, /device:TPU:0, one launch (start us, length us, event | category | flops | bytes accessed | tf_op | source)
XLA Modules:
  0.0 277.2 jit_solution(48984093554185324)
XLA Ops:
  1.9 5.3 %all-to-all-start = ((s32[8,1,8]{2,1,0:T(1,128)}), s32[8,1,8]{2,1,0:T(1,128)S(1)}, u32[]{:S(2)}, u32[]{:S(2)}) async-start(s32[8,1,8]{2,1,0:T(1,128)} %broadcast_in_dim.134), calls=%async_computation | async-start | bytes 8192 | tf_op jit(solution)/shard_map/all_to_all | solution.py:306
  7.2 6.8 %bitcast_bitcast_fusion = bf16[8,8,128,2,128]{4,3,2,1,0:T(2,128)(2,1)S(1)} fusion(bf16[8,128,2,1024]{3,2,1,0:T(2,128)(2,1)} %param.15), kind=kLoop, calls=%fused_computation.14 | loop fusion | bytes 8388608 | tf_op jit(solution)/shard_map/transpose | solution.py:297
  17.2 4.3 %fusion.12 = (bf16[8,4,128,2,128]{4,3,2,1,0:T(2,128)(2,1)}, bf16[8,4,128,2,128]{4,3,2,1,0:T(2,128)(2,1)}) fusion(bf16[8,8,128,2,128]{4,3,2,1,0:T(2,128)(2,1)S(1)} %slice_dynamic-update-slice_fusion), kind=kLoop, calls=%fused_computation.114 | loop fusion | bytes 8388608 | tf_op jit(solution)/shard_map/slice | solution.py:301
  21.6 4.4 %all-to-all-start.2 = ((bf16[8,4,128,2,128]{4,3,2,1,0:T(2,128)(2,1)}), bf16[8,4,128,2,128]{4,3,2,1,0:T(2,128)(2,1)}, u32[]{:S(2)}, u32[]{:S(2)}) async-start(bf16[8,4,128,2,128]{4,3,2,1,0:T(2,128)(2,1)} %get-tuple-element.43), calls=%async_computation.2 | async-start | bytes 4194304 | tf_op jit(solution)/shard_map/all_to_all | solution.py:302
  33.3 18.3 %all-to-all-done.2 = bf16[8,4,128,2,128]{4,3,2,1,0:T(2,128)(2,1)} async-done(((bf16[8,4,128,2,128]{4,3,2,1,0:T(2,128)(2,1)}), bf16[8,4,128,2,128]{4,3,2,1,0:T(2,128)(2,1)}, u32[]{:S(2)}, u32[]{:S(2)}) %all-to-all-start.2) | async-done | bytes 2097184 | tf_op jit(solution)/shard_map/all_to_all | solution.py:302
  51.7 4.7 %all-to-all-start.1 = ((bf16[8,4,128,2,128]{4,3,2,1,0:T(2,128)(2,1)}), bf16[8,4,128,2,128]{4,3,2,1,0:T(2,128)(2,1)}, u32[]{:S(2)}, u32[]{:S(2)}) async-start(bf16[8,4,128,2,128]{4,3,2,1,0:T(2,128)(2,1)} %get-tuple-element.44), calls=%async_computation.1 | async-start | bytes 4194304 | tf_op jit(solution)/shard_map/all_to_all | solution.py:302
  57.9 7.0 %gather_fusion.2 = bf16[4,128,2,1024]{3,2,1,0:T(2,128)(2,1)S(1)} fusion(bf16[8,128,2,1024]{3,2,1,0:T(2,128)(2,1)} %param.15, s32[1024]{0:T(1024)S(1)} %pad_clamp_fusion), kind=kCustom, calls=%fused_computation.8 | custom fusion | bytes 4194320 | tf_op jit(solution)/shard_map/gather | solution.py:374
  66.7 2.3 slice_bitcast_fusion.3
  80.8 38.0 %attend_first.1 = (f32[4,1024,256]{2,1,0:T(8,128)}, f32[4,1024,128]{2,1,0:T(8,128)}) custom-call(s32[32]{0:T(128)} %copy-done.13, s32[2]{0:T(128)} %pad_add_fusion.2.counts, bf16[8,4,256,128]{3,2,1,0:T(8,128)(2,1)} %bitcast.22.x_ref, bf16[4,1024,128]{2,1,0:T(8,128)(2,1)} %pad_maximum_fusion.q_ref, s32[4,128,1]{2,1,0:T(8,128)} %copy.39.qpos_ref, ...), custom_call_target="tpu_custom_call" | custom-call | flops 8589934592 | bytes 3145728 | tf_op jit(solution)/shard_map/attend_first/pallas_call | solution.py:175
  118.8 22.0 %attend_last.1 = (bf16[4,1024,128]{2,1,0:T(8,128)(2,1)}, f32[4,2,8,128]{3,2,1,0:T(8,128)}) custom-call(s32[32]{0:T(128)} %copy-done.14, s32[2]{0:T(128)} %pad_add_fusion.1.counts, bf16[8,4,256,128]{3,2,1,0:T(8,128)(2,1)} %bitcast.4.x_ref, bf16[4,1024,128]{2,1,0:T(8,128)(2,1)} %pad_maximum_fusion.q_ref, s32[4,128,1]{2,1,0:T(8,128)} %copy.39.qpos_ref, ...), custom_call_target="tpu_custom_call" | custom-call | flops 8589934592 | bytes 3145728 | tf_op jit(solution)/shard_map/attend_last/pallas_call | solution.py:175
  140.8 2.1 slice_bitcast_fusion.6
  143.5 4.0 %collective-permute-start.1 = (bf16[1024,128]{1,0:T(8,128)(2,1)S(1)}, bf16[1024,128]{1,0:T(8,128)(2,1)S(1)}, u32[]{:S(2)}, u32[]{:S(2)}) collective-permute-start(bf16[1024,128]{1,0:T(8,128)(2,1)S(1)} %get-tuple-element.52), channel_id=1, source_target_pairs={{0,1},{1,9},{2,3},{3,11},{4,5},{5,13},{6,7},{7,15},{8,0},{9,8},{10... | collective-permute-start | bytes 786440 | tf_op jit(solution)/shard_map/ppermute | solution.py:29
  153.4 7.1 %collective-permute-done.3.refs_3_ = f32[2,8,128]{2,1,0:T(8,128)S(1)} collective-permute-done((f32[2,8,128]{2,1,0:T(8,128)S(1)}, f32[2,8,128]{2,1,0:T(8,128)S(1)}, u32[]{:S(2)}, u32[]{:S(2)}) %collective-permute-start.3) | collective-permute-done | bytes 8224 | tf_op jit(solution)/shard_map/ppermute | solution.py:29
  166.0 10.9 %project.2 = (f32[64,8192]{1,0:T(8,128)}, bf16[64,8192]{1,0:T(8,128)(2,1)}) custom-call(bf16[1024,128]{1,0:T(8,128)(2,1)} %copy-done.2, bf16[1024,128]{1,0:T(8,128)(2,1)} %copy-done.3, f32[2,8,128]{2,1,0:T(8,128)} %copy-done.5, f32[2,8,128]{2,1,0:T(8,128)} %copy-done.6, bf16[512,8192]{1,0:T(8,128)(2,1)} %refs_4_.3, ...), custom_call_target="tpu_custom_call" | custom-call | flops 2147483648 | bytes 16777216 | tf_op jit(solution)/shard_map/project/pallas_call | solution.py:244
  178.5 6.3 %collective-permute-done.18 = bf16[128,2,1024]{2,1,0:T(2,128)(2,1)S(1)} collective-permute-done((bf16[128,2,1024]{2,1,0:T(2,128)(2,1)}, bf16[128,2,1024]{2,1,0:T(2,128)(2,1)S(1)}, u32[]{:S(2)}, u32[]{:S(2)}) %collective-permute-start.18) | collective-permute-done | bytes 524320 | tf_op jit(solution)/shard_map/ppermute | solution.py:29
  185.5 14.9 %collective-permute-done.19 = bf16[128,2,1024]{2,1,0:T(2,128)(2,1)S(1)} collective-permute-done((bf16[128,2,1024]{2,1,0:T(2,128)(2,1)S(1)}, bf16[128,2,1024]{2,1,0:T(2,128)(2,1)S(1)}, u32[]{:S(2)}, u32[]{:S(2)}) %collective-permute-start.19) | collective-permute-done | bytes 524320 | tf_op jit(solution)/shard_map/ppermute | solution.py:29
  200.4 10.5 %collective-permute-done.20 = bf16[128,2,1024]{2,1,0:T(2,128)(2,1)S(1)} collective-permute-done((bf16[128,2,1024]{2,1,0:T(2,128)(2,1)S(1)}, bf16[128,2,1024]{2,1,0:T(2,128)(2,1)S(1)}, u32[]{:S(2)}, u32[]{:S(2)}) %collective-permute-start.20) | collective-permute-done | bytes 524320 | tf_op jit(solution)/shard_map/ppermute | solution.py:29
  210.9 10.1 %broadcast_select_fusion.4 = bf16[8,128,2,1024]{3,2,1,0:T(2,128)(2,1)} fusion(pred[8]{0:T(512)(128)(4,1)S(1)} %get-tuple-element.90, pred[8]{0:T(512)(128)(4,1)S(1)} %get-tuple-element.89, pred[8]{0:T(512)(128)(4,1)S(1)} %get-tuple-element.88, pred[8]{0:T(512)(128)(4,1)S(1)} %get-tuple-element.87, bf16[8,128,2,1024]{3,2,1,0:T(2,128)(2,1)} %param.15, ...), kind=kLoop, calls=%fused_computation.13 | loop fusion | flops 10485760 | bytes 10485800 | tf_op jit(solution)/shard_map/jit(_where)/select_n | solution.py:274
  222.3 10.9 %project.3 = (f32[64,8192]{1,0:T(8,128)}, bf16[64,8192]{1,0:T(8,128)(2,1)}) custom-call(bf16[1024,128]{1,0:T(8,128)(2,1)} %copy-done.4, bf16[1024,128]{1,0:T(8,128)(2,1)} %collective-permute-done.10.refs_1_, f32[2,8,128]{2,1,0:T(8,128)} %copy-done.7, f32[2,8,128]{2,1,0:T(8,128)} %copy-done.8, bf16[512,8192]{1,0:T(8,128)(2,1)} %refs_4_.3, ...), custom_call_target="tpu_custom_call" | custom-call | flops 2147483648 | bytes 16777216 | tf_op jit(solution)/shard_map/project/pallas_call | solution.py:244
  235.8 4.3 %collective-permute-start.8 = (bf16[16,8192]{1,0:T(8,128)(2,1)S(1)}, bf16[16,8192]{1,0:T(8,128)(2,1)S(1)}, u32[]{:S(2)}, u32[]{:S(2)}) collective-permute-start(bf16[16,8192]{1,0:T(8,128)(2,1)S(1)} %get-tuple-element.50), channel_id=1, source_target_pairs={{0,12},{1,13},{2,14},{3,15},{4,8},{5,9},{6,10},{7,11},{8,4},{9,5},... | collective-permute-start | bytes 786440 | tf_op jit(solution)/shard_map/ppermute | solution.py:29
  240.1 13.1 %collective-permute-done.13 = bf16[64,8192]{1,0:T(8,128)(2,1)S(1)} collective-permute-done((bf16[64,8192]{1,0:T(8,128)(2,1)}, bf16[64,8192]{1,0:T(8,128)(2,1)S(1)}, u32[]{:S(2)}, u32[]{:S(2)}) %collective-permute-start.13) | collective-permute-done | bytes 1048608 | tf_op jit(solution)/shard_map/ppermute | solution.py:29
  253.7 4.2 %collective-permute-start.16 = (bf16[16,8192]{1,0:T(8,128)(2,1)S(1)}, bf16[16,8192]{1,0:T(8,128)(2,1)S(1)}, u32[]{:S(2)}, u32[]{:S(2)}) collective-permute-start(bf16[16,8192]{1,0:T(8,128)(2,1)S(1)} %get-tuple-element.57), channel_id=1, source_target_pairs={{0,12},{1,13},{2,14},{3,15},{4,8},{5,9},{6,10},{7,11},{8,4},{9,5},... | collective-permute-start | bytes 786440 | tf_op jit(solution)/shard_map/ppermute | solution.py:29
  258.1 3.8 %collective-permute-done.14 = bf16[16,8192]{1,0:T(8,128)(2,1)S(1)} collective-permute-done((bf16[16,8192]{1,0:T(8,128)(2,1)S(1)}, bf16[16,8192]{1,0:T(8,128)(2,1)S(1)}, u32[]{:S(2)}, u32[]{:S(2)}) %collective-permute-start.14) | collective-permute-done | bytes 262176 | tf_op jit(solution)/shard_map/ppermute | solution.py:29
  261.9 14.3 %collective-permute-done.15 = bf16[16,8192]{1,0:T(8,128)(2,1)S(1)} collective-permute-done((bf16[16,8192]{1,0:T(8,128)(2,1)S(1)}, bf16[16,8192]{1,0:T(8,128)(2,1)S(1)}, u32[]{:S(2)}, u32[]{:S(2)}) %collective-permute-start.15) | collective-permute-done | bytes 262176 | tf_op jit(solution)/shard_map/ppermute | solution.py:29
  (149 shorter events, 43.8 us)
Async XLA Ops:
  1.9 19.7 %all-to-all-start = ((s32[8,1,8]{2,1,0:T(1,128)}), s32[8,1,8]{2,1,0:T(1,128)S(1)}, u32[]{:S(2)}, u32[]{:S(2)}) async-start(s32[8,1,8]{2,1,0:T(1,128)} %broadcast_in_dim.134), calls=%async_computation | async-start | bytes 8192 | tf_op jit(solution)/shard_map/all_to_all | solution.py:306
  21.6 30.1 %all-to-all-start.2 = ((bf16[8,4,128,2,128]{4,3,2,1,0:T(2,128)(2,1)}), bf16[8,4,128,2,128]{4,3,2,1,0:T(2,128)(2,1)}, u32[]{:S(2)}, u32[]{:S(2)}) async-start(bf16[8,4,128,2,128]{4,3,2,1,0:T(2,128)(2,1)} %get-tuple-element.43), calls=%async_computation.2 | async-start | bytes 4194304 | tf_op jit(solution)/shard_map/all_to_all | solution.py:302
  26.0 138.4 %collective-permute-start.4 = (bf16[512,8192]{1,0:T(8,128)(2,1)}, bf16[512,8192]{1,0:T(8,128)(2,1)}, u32[]{:S(2)}, u32[]{:S(2)}) collective-permute-start(bf16[512,8192]{1,0:T(8,128)(2,1)} %refs_4_.3), channel_id=1, source_target_pairs={{0,1},{1,0},{2,3},{3,2},{4,5},{5,4},{6,7},{7,6},{8,9},{9,8},{10,11... | collective-permute-start | bytes 25165832 | tf_op jit(solution)/shard_map/ppermute | solution.py:29
  51.7 67.1 %all-to-all-start.1 = ((bf16[8,4,128,2,128]{4,3,2,1,0:T(2,128)(2,1)}), bf16[8,4,128,2,128]{4,3,2,1,0:T(2,128)(2,1)}, u32[]{:S(2)}, u32[]{:S(2)}) async-start(bf16[8,4,128,2,128]{4,3,2,1,0:T(2,128)(2,1)} %get-tuple-element.44), calls=%async_computation.1 | async-start | bytes 4194304 | tf_op jit(solution)/shard_map/all_to_all | solution.py:302
  142.8 19.1 %collective-permute-start = (bf16[1024,128]{1,0:T(8,128)(2,1)S(1)}, bf16[1024,128]{1,0:T(8,128)(2,1)S(1)}, u32[]{:S(2)}, u32[]{:S(2)}) collective-permute-start(bf16[1024,128]{1,0:T(8,128)(2,1)S(1)} %get-tuple-element.55), channel_id=1, source_target_pairs={{0,0},{1,8},{2,2},{3,10},{4,4},{5,12},{6,6},{7,14},{8,1},{9,9},{10... | collective-permute-start | bytes 786440 | tf_op jit(solution)/shard_map/ppermute | solution.py:29
  143.5 18.8 %collective-permute-start.1 = (bf16[1024,128]{1,0:T(8,128)(2,1)S(1)}, bf16[1024,128]{1,0:T(8,128)(2,1)S(1)}, u32[]{:S(2)}, u32[]{:S(2)}) collective-permute-start(bf16[1024,128]{1,0:T(8,128)(2,1)S(1)} %get-tuple-element.52), channel_id=1, source_target_pairs={{0,1},{1,9},{2,3},{3,11},{4,5},{5,13},{6,7},{7,15},{8,0},{9,8},{10... | collective-permute-start | bytes 786440 | tf_op jit(solution)/shard_map/ppermute | solution.py:29
  148.3 3.3 %collective-permute-start.2 = (f32[2,8,128]{2,1,0:T(8,128)S(1)}, f32[2,8,128]{2,1,0:T(8,128)S(1)}, u32[]{:S(2)}, u32[]{:S(2)}) collective-permute-start(f32[2,8,128]{2,1,0:T(8,128)S(1)} %get-tuple-element.62), channel_id=1, source_target_pairs={{0,0},{1,8},{2,2},{3,10},{4,4},{5,12},{6,6},{7,14},{8,1},{9,9},{10... | collective-permute-start | bytes 24584 | tf_op jit(solution)/shard_map/ppermute | solution.py:29
  149.0 11.6 %collective-permute-start.3 = (f32[2,8,128]{2,1,0:T(8,128)S(1)}, f32[2,8,128]{2,1,0:T(8,128)S(1)}, u32[]{:S(2)}, u32[]{:S(2)}) collective-permute-start(f32[2,8,128]{2,1,0:T(8,128)S(1)} %get-tuple-element.59), channel_id=1, source_target_pairs={{0,1},{1,9},{2,3},{3,11},{4,5},{5,13},{6,7},{7,15},{8,0},{9,8},{10... | collective-permute-start | bytes 24584 | tf_op jit(solution)/shard_map/ppermute | solution.py:29
  151.6 25.3 %collective-permute-start.17 = (bf16[128,2,1024]{2,1,0:T(2,128)(2,1)}, bf16[128,2,1024]{2,1,0:T(2,128)(2,1)S(1)}, u32[]{:S(2)}, u32[]{:S(2)}) collective-permute-start(bf16[128,2,1024]{2,1,0:T(2,128)(2,1)} %get-tuple-element.45), channel_id=1, source_target_pairs={{0,4},{1,5},{2,6},{3,7},{4,8},{5,9},{6,10},{7,11},{8,12},{9,13},{1... | collective-permute-start | bytes 1572872 | tf_op jit(solution)/shard_map/ppermute | solution.py:29
  160.5 24.3 %collective-permute-start.18 = (bf16[128,2,1024]{2,1,0:T(2,128)(2,1)}, bf16[128,2,1024]{2,1,0:T(2,128)(2,1)S(1)}, u32[]{:S(2)}, u32[]{:S(2)}) collective-permute-start(bf16[128,2,1024]{2,1,0:T(2,128)(2,1)} %get-tuple-element.47), channel_id=1, source_target_pairs={{0,3},{1,4},{2,5},{3,6},{4,7},{5,8},{6,9},{7,10},{8,11},{9,12},{10... | collective-permute-start | bytes 1572872 | tf_op jit(solution)/shard_map/ppermute | solution.py:29
  162.0 38.4 %collective-permute-start.19 = (bf16[128,2,1024]{2,1,0:T(2,128)(2,1)S(1)}, bf16[128,2,1024]{2,1,0:T(2,128)(2,1)S(1)}, u32[]{:S(2)}, u32[]{:S(2)}) collective-permute-start(bf16[128,2,1024]{2,1,0:T(2,128)(2,1)S(1)} %get-tuple-element.46), channel_id=1, source_target_pairs={{0,2},{1,3},{2,4},{3,5},{4,6},{5,7},{6,8},{7,9},{8,10},{9,11},{10,... | collective-permute-start | bytes 1572872 | tf_op jit(solution)/shard_map/ppermute | solution.py:29
  163.0 47.9 %collective-permute-start.20 = (bf16[128,2,1024]{2,1,0:T(2,128)(2,1)S(1)}, bf16[128,2,1024]{2,1,0:T(2,128)(2,1)S(1)}, u32[]{:S(2)}, u32[]{:S(2)}) collective-permute-start(bf16[128,2,1024]{2,1,0:T(2,128)(2,1)S(1)} %get-tuple-element.48), channel_id=1, source_target_pairs={{0,1},{1,2},{2,3},{3,4},{4,5},{5,6},{6,7},{7,8},{8,9},{9,10},{10,1... | collective-permute-start | bytes 1572872 | tf_op jit(solution)/shard_map/ppermute | solution.py:29
  164.3 56.7 %collective-permute-start.10 = (bf16[1024,128]{1,0:T(8,128)(2,1)}, bf16[1024,128]{1,0:T(8,128)(2,1)}, u32[]{:S(2)}, u32[]{:S(2)}) collective-permute-start(bf16[1024,128]{1,0:T(8,128)(2,1)} %get-tuple-element.53), channel_id=1, source_target_pairs={{0,1},{1,9},{2,3},{3,11},{4,5},{5,13},{6,7},{7,15},{8,0},{9,8},{10... | collective-permute-start | bytes 786440 | tf_op jit(solution)/shard_map/ppermute | solution.py:29
  176.9 44.2 %collective-permute-start.9 = (bf16[1024,128]{1,0:T(8,128)(2,1)}, bf16[1024,128]{1,0:T(8,128)(2,1)S(1)}, u32[]{:S(2)}, u32[]{:S(2)}) collective-permute-start(bf16[1024,128]{1,0:T(8,128)(2,1)} %get-tuple-element.54), channel_id=1, source_target_pairs={{0,0},{1,8},{2,2},{3,10},{4,4},{5,12},{6,6},{7,14},{8,1},{9,9},{10... | collective-permute-start | bytes 786440 | tf_op jit(solution)/shard_map/ppermute | solution.py:29
  184.8 36.2 %collective-permute-start.11 = (f32[2,8,128]{2,1,0:T(8,128)S(1)}, f32[2,8,128]{2,1,0:T(8,128)S(1)}, u32[]{:S(2)}, u32[]{:S(2)}) collective-permute-start(f32[2,8,128]{2,1,0:T(8,128)S(1)} %get-tuple-element.61), channel_id=1, source_target_pairs={{0,0},{1,8},{2,2},{3,10},{4,4},{5,12},{6,6},{7,14},{8,1},{9,9},{10... | collective-permute-start | bytes 24584 | tf_op jit(solution)/shard_map/ppermute | solution.py:29
  200.4 20.6 %collective-permute-start.12 = (f32[2,8,128]{2,1,0:T(8,128)S(1)}, f32[2,8,128]{2,1,0:T(8,128)S(1)}, u32[]{:S(2)}, u32[]{:S(2)}) collective-permute-start(f32[2,8,128]{2,1,0:T(8,128)S(1)} %get-tuple-element.60), channel_id=1, source_target_pairs={{0,1},{1,9},{2,3},{3,11},{4,5},{5,13},{6,7},{7,15},{8,0},{9,8},{10... | collective-permute-start | bytes 24584 | tf_op jit(solution)/shard_map/ppermute | solution.py:29
  210.9 24.4 %collective-permute-start.5 = (bf16[64,8192]{1,0:T(8,128)(2,1)}, bf16[64,8192]{1,0:T(8,128)(2,1)S(1)}, u32[]{:S(2)}, u32[]{:S(2)}) collective-permute-start(bf16[64,8192]{1,0:T(8,128)(2,1)} %get-tuple-element.22), channel_id=1, source_target_pairs={{0,2},{1,3},{2,0},{3,1},{4,6},{5,7},{6,4},{7,5},{8,10},{9,11},{10,... | collective-permute-start | bytes 3145736 | tf_op jit(solution)/shard_map/ppermute | solution.py:29
  233.2 20.0 %collective-permute-start.13 = (bf16[64,8192]{1,0:T(8,128)(2,1)}, bf16[64,8192]{1,0:T(8,128)(2,1)S(1)}, u32[]{:S(2)}, u32[]{:S(2)}) collective-permute-start(bf16[64,8192]{1,0:T(8,128)(2,1)} %get-tuple-element.24), channel_id=1, source_target_pairs={{0,2},{1,3},{2,0},{3,1},{4,6},{5,7},{6,4},{7,5},{8,10},{9,11},{10,... | collective-permute-start | bytes 3145736 | tf_op jit(solution)/shard_map/ppermute | solution.py:29
  235.6 18.1 %collective-permute-start.6 = (bf16[16,8192]{1,0:T(8,128)(2,1)S(1)}, bf16[16,8192]{1,0:T(8,128)(2,1)S(1)}, u32[]{:S(2)}, u32[]{:S(2)}) collective-permute-start(bf16[16,8192]{1,0:T(8,128)(2,1)S(1)} %get-tuple-element.49), channel_id=1, source_target_pairs={{0,4},{1,5},{2,6},{3,7},{4,0},{5,1},{6,2},{7,3},{8,12},{9,13},{10,... | collective-permute-start | bytes 786440 | tf_op jit(solution)/shard_map/ppermute | solution.py:29
  235.7 22.3 %collective-permute-start.7 = (bf16[16,8192]{1,0:T(8,128)(2,1)S(1)}, bf16[16,8192]{1,0:T(8,128)(2,1)S(1)}, u32[]{:S(2)}, u32[]{:S(2)}) collective-permute-start(bf16[16,8192]{1,0:T(8,128)(2,1)S(1)} %get-tuple-element.51), channel_id=1, source_target_pairs={{0,8},{1,9},{2,10},{3,11},{4,12},{5,13},{6,14},{7,15},{8,0},{9,1},... | collective-permute-start | bytes 786440 | tf_op jit(solution)/shard_map/ppermute | solution.py:29
  235.8 22.2 %collective-permute-start.8 = (bf16[16,8192]{1,0:T(8,128)(2,1)S(1)}, bf16[16,8192]{1,0:T(8,128)(2,1)S(1)}, u32[]{:S(2)}, u32[]{:S(2)}) collective-permute-start(bf16[16,8192]{1,0:T(8,128)(2,1)S(1)} %get-tuple-element.50), channel_id=1, source_target_pairs={{0,12},{1,13},{2,14},{3,15},{4,8},{5,9},{6,10},{7,11},{8,4},{9,5},... | collective-permute-start | bytes 786440 | tf_op jit(solution)/shard_map/ppermute | solution.py:29
  253.5 8.4 %collective-permute-start.14 = (bf16[16,8192]{1,0:T(8,128)(2,1)S(1)}, bf16[16,8192]{1,0:T(8,128)(2,1)S(1)}, u32[]{:S(2)}, u32[]{:S(2)}) collective-permute-start(bf16[16,8192]{1,0:T(8,128)(2,1)S(1)} %get-tuple-element.56), channel_id=1, source_target_pairs={{0,4},{1,5},{2,6},{3,7},{4,0},{5,1},{6,2},{7,3},{8,12},{9,13},{10,... | collective-permute-start | bytes 786440 | tf_op jit(solution)/shard_map/ppermute | solution.py:29
  253.6 22.6 %collective-permute-start.15 = (bf16[16,8192]{1,0:T(8,128)(2,1)S(1)}, bf16[16,8192]{1,0:T(8,128)(2,1)S(1)}, u32[]{:S(2)}, u32[]{:S(2)}) collective-permute-start(bf16[16,8192]{1,0:T(8,128)(2,1)S(1)} %get-tuple-element.58), channel_id=1, source_target_pairs={{0,8},{1,9},{2,10},{3,11},{4,12},{5,13},{6,14},{7,15},{8,0},{9,1},... | collective-permute-start | bytes 786440 | tf_op jit(solution)/shard_map/ppermute | solution.py:29
  253.7 22.5 %collective-permute-start.16 = (bf16[16,8192]{1,0:T(8,128)(2,1)S(1)}, bf16[16,8192]{1,0:T(8,128)(2,1)S(1)}, u32[]{:S(2)}, u32[]{:S(2)}) collective-permute-start(bf16[16,8192]{1,0:T(8,128)(2,1)S(1)} %get-tuple-element.57), channel_id=1, source_target_pairs={{0,12},{1,13},{2,14},{3,15},{4,8},{5,9},{6,10},{7,11},{8,4},{9,5},... | collective-permute-start | bytes 786440 | tf_op jit(solution)/shard_map/ppermute | solution.py:29
  (15 other events, 171.4 us)

commit v2 on v1

v2 whole, which is shorter than its diff:
```python
import functools

import jax
import jax.numpy as jnp
from jax import lax
from jax.experimental import pallas as pl
from jax.experimental.pallas import tpu as pltpu
from jax.sharding import PartitionSpec as P

HEADS = 64
KV_HEADS = 8
HEAD_DIM = 128
D = 8192
PAGE_TOK = 128
BLOCK = 256
MOVE_WIN = 4
GROUP = HEADS // KV_HEADS

FLOOR = -1e30
FAR = 1 << 30
SCALE = HEAD_DIM**-0.5 * 1.4426950408889634

WIDE = 16
NARROW = 8
FIRST_SLOTS = 5
COLUMN_PARTS = 2

ANY = pl.BlockSpec(memory_space=pl.ANY)


def permute_to(x, n, target):
    return lax.ppermute(x, "pages", [(i, target(i)) for i in range(n)])


def head_of(j):
    half = KV_HEADS // 2
    return (j % 2) * half + j // 2


def split_heads_kernel(kv_ref, out_ref, sems, *, first):
    copies = []
    for d in range(KV_HEADS):
        copies.append(
            pltpu.make_async_copy(
                kv_ref.at[
                    pl.ds(first, out_ref.shape[1]),
                    :,
                    :,
                    pl.ds(head_of(d) * HEAD_DIM, HEAD_DIM),
                ],
                out_ref.at[d],
                sems.at[d],
            )
        )
    for copy in copies:
        copy.start()
    for copy in copies:
        copy.wait()


def split_heads(kv_cache, first, count):
    return pl.pallas_call(
        functools.partial(split_heads_kernel, first=first),
        out_shape=jax.ShapeDtypeStruct(
            (KV_HEADS, count, PAGE_TOK, 2, HEAD_DIM), kv_cache.dtype
        ),
        in_specs=[ANY],
        out_specs=ANY,
        scratch_shapes=[pltpu.SemaphoreType.DMA((KV_HEADS,))],
        name="split_heads",
    )(kv_cache)


def outgoing_kernel(move_out, kv_ref, after_ref, *refs):
    outs, sems = refs[:MOVE_WIN], refs[MOVE_WIN]
    copies = [
        pltpu.make_async_copy(
            kv_ref.at[jnp.maximum(move_out[o], 0)], outs[o], sems.at[o]
        )
        for o in range(MOVE_WIN)
    ]
    for copy in copies:
        copy.start()
    for copy in copies:
        copy.wait()


def outgoing_pages(kv_cache, move_out, after):
    page = jax.ShapeDtypeStruct(kv_cache.shape[1:], kv_cache.dtype)
    return pl.pallas_call(
        outgoing_kernel,
        out_shape=(page,) * MOVE_WIN,
        grid_spec=pltpu.PrefetchScalarGridSpec(
            num_scalar_prefetch=1,
            grid=(),
            in_specs=[ANY, ANY],
            out_specs=(ANY,) * MOVE_WIN,
            scratch_shapes=[pltpu.SemaphoreType.DMA((MOVE_WIN,))],
        ),
        name="outgoing_pages",
    )(move_out, kv_cache, after)


def arrange_kernel(page_after, move_in, kv_ref, *refs):
    arrived = refs[:MOVE_WIN]
    _, out_ref, zero_ref, sems = refs[MOVE_WIN:]
    zero_ref[...] = jnp.zeros(zero_ref.shape, zero_ref.dtype)
    slots = out_ref.shape[0]
    for s in range(slots):
        taken = jnp.zeros((), jnp.bool_)
        for o in reversed(range(MOVE_WIN)):
            lands = move_in[o] == s

            @pl.when(lands & jnp.logical_not(taken))
            def _():
                pltpu.make_async_copy(arrived[o], out_ref.at[s], sems.at[s]).start()

            taken = taken | lands
        kept = page_after[s] >= 0

        @pl.when(kept & jnp.logical_not(taken))
        def _():
            pltpu.make_async_copy(kv_ref.at[s], out_ref.at[s], sems.at[s]).start()

        @pl.when(jnp.logical_not(kept | taken))
        def _():
            pltpu.make_async_copy(zero_ref, out_ref.at[s], sems.at[s]).start()

    for s in range(slots):
        pltpu.make_async_copy(kv_ref.at[s], out_ref.at[s], sems.at[s]).wait()


def arrange_pages(kv_cache, arrived, page_after, move_in, after):
    return pl.pallas_call(
        arrange_kernel,
        out_shape=jax.ShapeDtypeStruct(kv_cache.shape, kv_cache.dtype),
        grid_spec=pltpu.PrefetchScalarGridSpec(
            num_scalar_prefetch=2,
            grid=(),
            in_specs=[ANY] * (2 + MOVE_WIN),
            out_specs=ANY,
            scratch_shapes=[
                pltpu.VMEM(kv_cache.shape[1:], kv_cache.dtype),
                pltpu.SemaphoreType.DMA((kv_cache.shape[0],)),
            ],
        ),
        name="arrange_pages",
    )(page_after, move_in, kv_cache, *arrived, after)


def three_parts(x):
    high = x.astype(jnp.bfloat16)
    rest = x - high.astype(jnp.float32)
    mid = rest.astype(jnp.bfloat16)
    low = (rest - mid.astype(jnp.float32)).astype(jnp.bfloat16)
    return high, mid, low


def attend_kernel(
    pages, place, x_ref, q_ref, *refs, first, last, rows, tok, ways, tok_rows, block
):
    n_in = 0 if first else 2
    carried = refs[:n_in]
    outs = refs[n_in : n_in + (1 if last else 2)]
    k_s, v_s, acc_s, m_s, order, counts = refs[n_in + len(outs) :]
    step = pl.program_id(0)
    src_slots = x_ref.shape[1]
    n_slots = x_ref.shape[0] * src_slots
    head, way = place[0], place[1]

    @pl.when(step == 0)
    def _():
        lowest = jnp.minimum(place[2], place[3])

        def fully(page):
            return (page >= 0) & (page * PAGE_TOK + (PAGE_TOK - 1) <= lowest)

        def put_full(i, count):
            yes = fully(pages[i])

            @pl.when(yes)
            def _():
                order[count] = i

            return count + yes.astype(jnp.int32)

        def put_rest(i, count):
            yes = (pages[i] >= 0) & jnp.logical_not(fully(pages[i]))

            @pl.when(yes)
            def _():
                order[count] = i

            return count + yes.astype(jnp.int32)

        n_full = lax.fori_loop(0, n_slots, put_full, 0)
        n_live = lax.fori_loop(0, n_slots, put_rest, n_full)
        counts[0] = n_full
        counts[1] = n_live

        row = lax.broadcasted_iota(jnp.int32, (2 * PAGE_TOK, 2 * PAGE_TOK), 0)
        col = lax.broadcasted_iota(jnp.int32, (2 * PAGE_TOK, 2 * PAGE_TOK), 1)
        want = jnp.where(row < PAGE_TOK, 2 * row, 2 * (row - PAGE_TOK) + 1)
        pick = jnp.where(col == want, 1.0, 0.0).astype(jnp.bfloat16)
        ones = jnp.ones((PAGE_TOK, HEAD_DIM), jnp.bfloat16)

        def split_step(i, carry):
            for s in range(NARROW):
                at = i * NARROW + s
                slot = order[jnp.minimum(at, n_live - 1)]
                both = jnp.dot(
                    pick,
                    x_ref[slot // src_slots, slot % src_slots],
                    preferred_element_type=jnp.float32,
                ).astype(jnp.bfloat16)
                to = pl.ds(pl.multiple_of(at * PAGE_TOK, PAGE_TOK), PAGE_TOK)
                k_s[to, :] = both[:PAGE_TOK]
                v_s[to, :HEAD_DIM] = both[PAGE_TOK:]
                v_s[to, HEAD_DIM:] = ones
            return carry

        lax.fori_loop(0, (n_live + NARROW - 1) // NARROW, split_step, 0)

    n_full, n_live = counts[0], counts[1]
    total = GROUP * tok
    if first:
        m_s[...] = jnp.full(m_s.shape, FLOOR, jnp.float32)
        acc_s[...] = jnp.zeros(acc_s.shape, jnp.float32)
    else:
        acc_s[...] = carried[0][0]
        m_s[...] = carried[1][0]

    if block is None:
        t_rel, b = step // 2, step % 2
    else:
        t_rel, b = step, block
    line = lax.broadcasted_iota(jnp.int32, (tok, PAGE_TOK), 0)
    p = line // tok_rows
    kx = (p % (KV_HEADS // 2)) * 2 + p // (KV_HEADS // 2)
    token = ((kx ^ head) * ways + (t_rel ^ way)) * tok_rows + line % tok_rows
    q_at = token + jnp.where(b == 0, place[2], place[3])

    def tile_step(at, size, masked):
        span_k = pl.ds(pl.multiple_of(at * PAGE_TOK, PAGE_TOK), size * PAGE_TOK)
        keys = k_s[span_k, :]
        values = v_s[span_k, :]
        if masked:
            lane = lax.broadcasted_iota(jnp.int32, (tok, PAGE_TOK), 1)
            visible = []
            for s in range(size):
                slot = order[jnp.minimum(at + s, n_live - 1)]
                start = jnp.where(at + s < n_live, pages[slot] * PAGE_TOK, FAR)
                seen = lane + start <= q_at
                visible.append(jnp.concatenate([seen] * (rows // tok), axis=0))

        def score(part):
            return lax.dot_general(
                q_ref[0, part * rows : (part + 1) * rows, :],
                keys,
                (((1,), (1,)), ((), ())),
                preferred_element_type=jnp.float32,
            )

        def soften(part, scores):
            span = slice(part * rows, (part + 1) * rows)
            pieces = [scores[:, s * PAGE_TOK : (s + 1) * PAGE_TOK] for s in range(size)]
            if masked:
                pieces = [jnp.where(v, x, FLOOR) for v, x in zip(visible, pieces)]
            peak = functools.reduce(jnp.maximum, pieces)
            m_old = m_s[span, :]
            m_new = jnp.maximum(m_old, jnp.max(peak, axis=1, keepdims=True) * SCALE)
            shift = jnp.maximum(m_new, 0.5 * FLOOR * SCALE) if masked else m_new
            weights = jnp.concatenate(
                [jnp.exp2(x * SCALE - shift).astype(jnp.bfloat16) for x in pieces], axis=1
            )
            m_s[span, :] = m_new
            return weights, jnp.exp2(m_old - m_new)

        def gather(part, weights, alpha):
            span = slice(part * rows, (part + 1) * rows)
            mixed = jnp.dot(weights, values, preferred_element_type=jnp.float32)
            acc_s[span, :HEAD_DIM] = acc_s[span, :HEAD_DIM] * alpha + mixed[:, :HEAD_DIM]
            acc_s[span, HEAD_DIM:] = acc_s[span, HEAD_DIM:] * alpha + mixed[:, HEAD_DIM:]

        parts = total // rows
        scores = score(0)
        waiting = None
        for part in range(parts):
            following = score(part + 1) if part + 1 < parts else None
            weights, alpha = soften(part, scores)
            if waiting is not None:
                gather(*waiting)
            waiting = (part, weights, alpha)
            scores = following
        gather(*waiting)

    n_wide = n_full // WIDE
    n_open = (n_full - n_wide * WIDE) // NARROW
    base = n_wide * WIDE
    done = base + n_open * NARROW
    n_masked = (n_live - done + NARROW - 1) // NARROW

    def wide(i, carry):
        tile_step(i * WIDE, WIDE, False)
        return carry

    def narrow(i, carry):
        tile_step(base + i * NARROW, NARROW, False)
        return carry

    def masked(i, carry):
        tile_step(done + i * NARROW, NARROW, True)
        return carry

    lax.fori_loop(0, n_wide, wide, 0)
    lax.fori_loop(0, n_open, narrow, 0)
    lax.fori_loop(0, n_masked, masked, 0)

    if not last:
        outs[0][0] = acc_s[...]
        outs[1][0] = m_s[...]
    else:
        out_ref = outs[0]
        out_ref[0, :total, :] = acc_s[:, :HEAD_DIM].astype(jnp.bfloat16)
        row = lax.broadcasted_iota(jnp.int32, (tok, HEAD_DIM), 0)
        col = lax.broadcasted_iota(jnp.int32, (tok, HEAD_DIM), 1)
        eye = row == col
        lines = []
        for ref, lanes in ((m_s, slice(0, HEAD_DIM)), (acc_s, slice(HEAD_DIM, 2 * HEAD_DIM))):
            for g in range(GROUP):
                span = slice(g * tok, (g + 1) * tok)
                lines.append(
                    jnp.sum(jnp.where(eye, ref[span, lanes], 0.0), axis=0, keepdims=True)
                )
        stats = jnp.concatenate(lines, axis=0)
        for i, piece in enumerate(three_parts(stats)):
            at = total + i * 2 * GROUP
            out_ref[0, at : at + 2 * GROUP, :] = piece


def attend(pages, place, x, q, carried, block, tok_rows, rows):
    sources, src_slots = x.shape[:2]
    steps, total, _ = q.shape
    tok = total // GROUP
    first = carried is None
    last = block is not None
    ways = steps // 2
    pad = WIDE - 1
    n_slots = -(-sources * src_slots // WIDE) * WIDE
    if last:
        grid = ways
        at = lambda i, *_: (2 * i + block, 0, 0)
    else:
        grid = steps
        at = lambda i, *_: (i, 0, 0)
    straight = lambda i, *_: (i, 0, 0)
    in_specs = [
        pl.BlockSpec(x.shape, lambda i, *_: (0, 0, 0, 0)),
        pl.BlockSpec((1, total, HEAD_DIM), at),
    ]
    sent = total + 3 * 2 * GROUP
    if last:
        out_shape = (jax.ShapeDtypeStruct((ways, sent, HEAD_DIM), jnp.bfloat16),)
        out_specs = (pl.BlockSpec((1, sent, HEAD_DIM), straight),)
    else:
        out_shape = (
            jax.ShapeDtypeStruct((steps, total, 2 * HEAD_DIM), jnp.float32),
            jax.ShapeDtypeStruct((steps, total, HEAD_DIM), jnp.float32),
        )
        out_specs = (
            pl.BlockSpec((1, total, 2 * HEAD_DIM), at),
            pl.BlockSpec((1, total, HEAD_DIM), at),
        )
    extra = ()
    if not first:
        extra = tuple(carried)
        in_specs += [
            pl.BlockSpec((1, total, 2 * HEAD_DIM), at),
            pl.BlockSpec((1, total, HEAD_DIM), at),
        ]
    flops = 8 * grid * total * sources * src_slots * PAGE_TOK * HEAD_DIM
    return pl.pallas_call(
        functools.partial(
            attend_kernel,
            first=first,
            last=last,
            rows=rows,
            tok=tok,
            ways=ways,
            tok_rows=tok_rows,
            block=block,
        ),
        out_shape=out_shape,
        grid_spec=pltpu.PrefetchScalarGridSpec(
            num_scalar_prefetch=2,
            grid=(grid,),
            in_specs=in_specs,
            out_specs=out_specs,
            scratch_shapes=[
                pltpu.VMEM((n_slots * PAGE_TOK, HEAD_DIM), jnp.bfloat16),
                pltpu.VMEM((n_slots * PAGE_TOK, 2 * HEAD_DIM), jnp.bfloat16),
                pltpu.VMEM((total, 2 * HEAD_DIM), jnp.float32),
                pltpu.VMEM((total, HEAD_DIM), jnp.float32),
                pltpu.SMEM((n_slots,), jnp.int32),
                pltpu.SMEM((2,), jnp.int32),
            ],
        ),
        cost_estimate=pl.CostEstimate(
            flops=flops, transcendentals=flops // (8 * HEAD_DIM), bytes_accessed=x.size * 2
        ),
        name="attend_last" if last else "attend_first",
    )(pages, place, x, q, *extra)


def merge(parts, a_ref, tok):
    total = GROUP * tok
    row = lax.broadcasted_iota(jnp.int32, (tok, HEAD_DIM), 0)
    col = lax.broadcasted_iota(jnp.int32, (tok, HEAD_DIM), 1)
    eye = row == col
    stats = []
    for part in parts:
        pieces = [
            part[total + i * 2 * GROUP : total + (i + 1) * 2 * GROUP, :].astype(jnp.float32)
            for i in range(3)
        ]
        stats.append((pieces[0] + pieces[1]) + pieces[2])
    tops = functools.reduce(jnp.maximum, [s[:GROUP] for s in stats])
    factors = [jnp.exp2(s[:GROUP] - tops) for s in stats]
    totals = sum(f * s[GROUP:] for f, s in zip(factors, stats))
    for g in range(GROUP):
        span = slice(g * tok, (g + 1) * tok)
        mixed = 0.0
        for f, part in zip(factors, parts):
            ratio = jnp.where(eye, f[g : g + 1] / totals[g : g + 1], 0.0)
            mixed += jnp.sum(ratio, axis=1, keepdims=True) * part[span, :].astype(jnp.float32)
        a_ref[:, g * HEAD_DIM : (g + 1) * HEAD_DIM] = mixed.astype(jnp.bfloat16)


def project_kernel(*refs, n_parts, n_ws, tok):
    parts = refs[:n_parts]
    ws = refs[n_parts : n_parts + n_ws]
    outs = refs[n_parts + n_ws :]
    keep_ref, send_ref = outs[:2]
    if n_parts == n_ws:
        a_ref = outs[2]

        @pl.when(pl.program_id(0) == 0)
        def _():
            merge(parts, a_ref, tok)

    else:
        a_ref = parts[0]
    depth = a_ref.shape[1] // n_ws
    total = 0.0
    for s in range(n_ws):
        total += jnp.dot(
            a_ref[:, s * depth : (s + 1) * depth], ws[s][...], preferred_element_type=jnp.float32
        )
    half = tok // 2
    keep_ref[...] = total[:half]
    send_ref[...] = total[half:].astype(jnp.bfloat16)


def project(parts, ws, tok, column_part, width=1024):
    columns = ws[0].shape[1] // COLUMN_PARTS
    steps = columns // width
    fixed = lambda i: (0, 0)
    half = tok // 2
    depth = sum(w.shape[0] for w in ws)
    merging = len(parts) == len(ws)
    out_shape = [
        jax.ShapeDtypeStruct((half, columns), jnp.float32),
        jax.ShapeDtypeStruct((half, columns), jnp.bfloat16),
    ]
    out_specs = [
        pl.BlockSpec((half, width), lambda i: (0, i)),
        pl.BlockSpec((half, width), lambda i: (0, i)),
    ]
    if merging:
        out_shape.append(jax.ShapeDtypeStruct((tok, depth), jnp.bfloat16))
        out_specs.append(pl.BlockSpec((tok, depth), fixed))
    return pl.pallas_call(
        functools.partial(project_kernel, n_parts=len(parts), n_ws=len(ws), tok=tok),
        out_shape=out_shape,
        grid=(steps,),
        in_specs=[pl.BlockSpec(o.shape, fixed) for o in parts]
        + [
            pl.BlockSpec((w.shape[0], width), lambda i: (0, column_part * steps + i)) for w in ws
        ],
        out_specs=out_specs,
        cost_estimate=pl.CostEstimate(
            flops=2 * tok * depth * columns, transcendentals=0, bytes_accessed=2 * depth * columns
        ),
        name="project",
    )(*parts, *ws)


def local(
    queries, kv_cache, w_out, slot_page_before, slot_page_after, move_out, move_in, positions
):
    n = lax.axis_size("pages")
    slots = kv_cache.shape[0]
    ways = n // KV_HEADS
    tok_rows = BLOCK // n
    tok = BLOCK // ways
    gp = GROUP // ways
    me = lax.axis_index("pages")
    way = me // KV_HEADS
    head = head_of(me % KV_HEADS)
    groups = [[a * KV_HEADS + b for b in range(KV_HEADS)] for a in range(ways)]

    def exchange(x):
        return lax.all_to_all(x, "pages", 0, 0, axis_index_groups=groups, tiled=True)

    cuts = [(0, FIRST_SLOTS), (FIRST_SLOTS, slots - FIRST_SLOTS)]
    pieces = [split_heads(kv_cache, at, count) for at, count in cuts]
    arrived = [
        exchange(piece).reshape(KV_HEADS, count, 2 * PAGE_TOK, HEAD_DIM)
        for piece, (_, count) in zip(pieces, cuts)
    ]
    table_in, _ = lax.optimization_barrier((slot_page_before, pieces[0]))
    table = exchange(jnp.broadcast_to(table_in[None, None], (KV_HEADS, 1, slots)))
    table = table.reshape(KV_HEADS, slots)
    place = jnp.stack([head, way, positions[0, 0], positions[1, 0]]).astype(jnp.int32)

    xs = lambda m: jnp.arange(m, dtype=jnp.int32)
    t_of = way ^ xs(ways)
    kx = (xs(KV_HEADS) % (KV_HEADS // 2)) * 2 + xs(KV_HEADS) // (KV_HEADS // 2)
    owner = (kx[None, :] ^ head) * ways + t_of[:, None]
    g_of = ((xs(GROUP) // gp)[None, :] ^ t_of[:, None]) * gp + (xs(GROUP) % gp)[None, :]
    mine = lax.dynamic_slice_in_dim(queries, head * GROUP * HEAD_DIM, GROUP * HEAD_DIM, axis=2)
    mine = mine.reshape(2, n, tok_rows, GROUP, HEAD_DIM)
    q_rows = []
    for tx in range(ways):
        taken = jnp.take(jnp.take(mine, owner[tx], axis=1), g_of[tx], axis=3)
        q_rows.append(jnp.transpose(taken, (0, 3, 1, 2, 4)).reshape(2, GROUP * tok, HEAD_DIM))
    q = jnp.concatenate(q_rows, axis=0)

    rows = 2 * tok
    pages = [table[:, at : at + count].reshape(-1) for at, count in cuts]
    carried = attend(pages[0], place, arrived[0], q, None, None, tok_rows, rows)

    leaving = outgoing_pages(kv_cache, move_out[0], arrived[0])
    landed = [
        permute_to(leaving[o - 1], n, lambda i: (i + o) % n) for o in range(1, MOVE_WIN + 1)
    ]

    ws = [w_out] + [permute_to(w_out, n, lambda i: i ^ s) for s in range(1, ways)]

    def merger(i, s):
        return head_of(i % KV_HEADS) * ways + ((i // KV_HEADS) ^ s)

    partial = []
    for b in range(2):
        (out,) = attend(pages[1], place, arrived[1], q, carried, b, tok_rows, rows)
        partial.append([permute_to(out[s], n, lambda i: merger(i, s)) for s in range(ways)])

    results = []
    for b in range(2):
        merged = partial[b]
        columns = []
        for c in range(COLUMN_PARTS):
            keep, send, *a = project(merged, ws, tok, c)
            if a:
                merged = a
            got = permute_to(send, n, lambda i: i ^ ways)
            total = (keep + got.astype(jnp.float32)).reshape(KV_HEADS // 2, tok_rows, -1)
            mine_rows = total[0]
            for zx in range(1, KV_HEADS // 2):
                got = permute_to(
                    total[zx].astype(jnp.bfloat16), n, lambda i: i ^ (zx * 2 * ways)
                )
                mine_rows = mine_rows + got.astype(jnp.float32)
            columns.append(mine_rows.astype(jnp.bfloat16))
        results.append(jnp.concatenate(columns, axis=1))

    cache_after = arrange_pages(kv_cache, landed, slot_page_after, move_in[0], send)
    return (jnp.stack(results), cache_after)


def solution(mesh):
    in_specs = (
        P(None, "groups", None),
        P(("groups", "pages"), None, None, None),
        P("pages", None),
        P(("groups", "pages")),
        P(("groups", "pages")),
        P(("groups", "pages"), None),
        P(("groups", "pages"), None),
        P(None, "groups"),
    )
    out_specs = (P(None, ("groups", "pages"), None), P(("groups", "pages"), None, None, None))
    return jax.shard_map(local, mesh=mesh, in_specs=in_specs, out_specs=out_specs, check_vma=False)
```

time: 282 us -> 508 us (1.80)
  Pallas kernels: 81.7 us -> 385 us
  waiting for transfers between devices: 88.5 us -> 13.1 us
  local copies, waits for them, and re-layouts: 39.3 us -> 17.9 us
  starting transfers between devices: 40 us -> 60.2 us
  other arithmetic: 23.9 us -> 12.6 us
  blocking collectives: 0 us -> 9.76 us
    pallas_call x4 -> x11, Pallas kernels: 81.7 us -> 385 us  [the longest x2 129 us: split_heads(): pl.pallas_call(functools.partial(split_heads_kernel, first=first), out_sh...]
    ppermute x21 -> x25, waiting for transfers between devices: 70.2 us -> 13.1 us  [permute_to(): return lax.ppermute(x, 'pages', [(i, target(i)) for i in range(n)])]
    ppermute x21 -> x25, starting transfers between devices: 25.7 us -> 52.3 us  [permute_to(): return lax.ppermute(x, 'pages', [(i, target(i)) for i in range(n)])]
    all_to_all x3 -> x2, waiting for transfers between devices: 18.3 us -> 0.01 us  [exchange(): lax.all_to_all(x, 'pages', 0, 0, axis_index_groups=groups, tiled=True)]
    select_n x6 -> x0, other arithmetic: 10.9 us -> none  [the longest x1 10.1 us: migrate_pages(): arranged = jnp.where(landing, arrived[None], arranged)]
    all_to_all x0 -> x1, blocking collectives: none -> 9.76 us  [exchange(): lax.all_to_all(x, 'pages', 0, 0, axis_index_groups=groups, tiled=True)]
    gather x5 -> x0, local copies, waits for them, and re-layouts: 9.59 us -> none  [the longest x1 7.04 us: local(): outgoing = kv_cache[jnp.maximum(move_out[0], 0)]]
    transpose x1 -> x0, local copies, waits for them, and re-layouts: 6.78 us -> none  [local(): by_head = jnp.transpose(by_head, (3, 0, 1, 2, 4))]
  transfers between devices with their start and end apart: 24 -> 27, of which waited for: 8 -> 5; matrix products, arithmetic and copies ran while one was open for 21% -> 6% of each run, Pallas kernels for 29% -> 61%
where the time goes in v2:
time: 508 us; the launch traced here: 499 us
  Pallas kernels  385 us (76%)
  starting transfers between devices  60.2 us (12%)
  local copies, waits for them, and re-layouts  17.9 us (4%)
  waiting for transfers between devices  13.1 us (3%)
  other arithmetic  12.6 us (2%)
  blocking collectives  9.76 us (2%)
    pallas_call x2, Pallas kernels, split_heads(): pl.pallas_call(functools.partial(split_heads_kernel, first=first), out_sh...  129 us
    pallas_call x1, Pallas kernels, arrange_pages(): pl.pallas_call(arrange_kernel, out_shape=jax.ShapeDtypeStruct(kv_cache.sh...  113 us
    pallas_call x1, Pallas kernels, outgoing_pages(): pl.pallas_call(outgoing_kernel, out_shape=(page,) * MOVE_WIN, grid_spec=p...  65.3 us
    ppermute x25, starting transfers between devices, permute_to(): return lax.ppermute(x, 'pages', [(i, target(i)) for i in range(n)])  52.3 us
    pallas_call x3, Pallas kernels, attend(): pl.pallas_call(functools.partial(attend_kernel, first=first, last=last, r...  51.7 us
    pallas_call x4, Pallas kernels, project(): pl.pallas_call(functools.partial(project_kernel, n_parts=len(parts), n_ws...  24.9 us
    ppermute x25, waiting for transfers between devices, permute_to(): return lax.ppermute(x, 'pages', [(i, target(i)) for i in range(n)])  13.1 us
  transfers between devices with their start and end apart: 27, of which 5 were waited for; matrix products, arithmetic and copies ran while one was open for 6% of the time, Pallas kernels for 61%

profile of v2, /device:TPU:0, one launch (start us, length us, event | category | flops | bytes accessed | tf_op | source)
XLA Modules:
  0.0 499.3 jit_solution(14854869068855823351)
XLA Ops:
  0.6 80.6 %split_heads.2 = bf16[8,5,128,2,128]{4,3,2,1,0:T(2,128)(2,1)} custom-call(bf16[8,128,2,1024]{3,2,1,0:T(2,128)(2,1)} %kv_ref.7), custom_call_target="tpu_custom_call" | custom-call | tf_op jit(solution)/shard_map/split_heads/pallas_call | solution.py:62
  81.3 9.8 %all_to_all.15 = s32[8,1,8]{2,1,0:T(1,128)S(1)} all-to-all(s32[8,1,8]{2,1,0:T(1,128)S(1)} %broadcast_in_dim.17), channel_id=1, replica_groups={{0,1,2,3,4,5,6,7},{8,9,10,11,12,13,14,15},{16,17,18,19,20,21,22,23},{24..., dimensions={0} | all-to-all | bytes 512 | tf_op jit(solution)/shard_map/all_to_all | solution.py:513
  91.0 3.6 all-to-all-start.2
  95.1 48.8 %split_heads.3 = bf16[8,3,128,2,128]{4,3,2,1,0:T(2,128)(2,1)} custom-call(bf16[8,128,2,1024]{3,2,1,0:T(2,128)(2,1)} %kv_ref.7), custom_call_target="tpu_custom_call" | custom-call | tf_op jit(solution)/shard_map/split_heads/pallas_call | solution.py:62
  148.5 2.7 gather_fusion
  154.1 4.3 all-to-all-start.1
  169.2 35.2 %attend_first.1 = (f32[4,1024,256]{2,1,0:T(8,128)}, f32[4,1024,128]{2,1,0:T(8,128)}) custom-call(s32[40]{0:T(128)} %reshape.119.pages, s32[4]{0:T(128)} %pad_add_fusion.place, bf16[8,5,256,128]{3,2,1,0:T(8,128)(2,1)} %bitcast.52, bf16[4,1024,128]{2,1,0:T(8,128)(2,1)} %pad_maximum_fusion.q_ref), custom_call_target="tpu_custom_call" | custom-call | flops 21474836480 | bytes 2621440 | tf_op jit(solution)/shard_map/attend_first/pallas_call | solution.py:382
  204.4 8.2 %attend_last.3 = bf16[2,1072,128]{2,1,0:T(8,128)(2,1)} custom-call(s32[24]{0:T(128)} %reshape.114.pages, s32[4]{0:T(128)} %pad_add_fusion.place, bf16[8,3,256,128]{3,2,1,0:T(8,128)(2,1)} %bitcast.5.x_ref, bf16[4,1024,128]{2,1,0:T(8,128)(2,1)} %pad_maximum_fusion.q_ref, f32[4,1024,256]{2,1,0:T(8,128)} %get-tuple-element.22.refs_0_, ...), custom_call_target="tpu_custom_call" | custom-call | flops 6442450944 | bytes 1572864 | tf_op jit(solution)/shard_map/attend_last/pallas_call | solution.py:382
  214.8 8.3 %attend_last.2 = bf16[2,1072,128]{2,1,0:T(8,128)(2,1)} custom-call(s32[24]{0:T(128)} %reshape.114.pages, s32[4]{0:T(128)} %pad_add_fusion.place, bf16[8,3,256,128]{3,2,1,0:T(8,128)(2,1)} %bitcast.5.x_ref, bf16[4,1024,128]{2,1,0:T(8,128)(2,1)} %pad_maximum_fusion.q_ref, f32[4,1024,256]{2,1,0:T(8,128)} %get-tuple-element.22.refs_0_, ...), custom_call_target="tpu_custom_call" | custom-call | flops 6442450944 | bytes 1572864 | tf_op jit(solution)/shard_map/attend_last/pallas_call | solution.py:382
  224.9 3.9 collective-permute-start.1
  230.4 65.3 %outgoing_pages.1 = (bf16[128,2,1024]{2,1,0:T(2,128)(2,1)}, bf16[128,2,1024]{2,1,0:T(2,128)(2,1)}, bf16[128,2,1024]{2,1,0:T(2,128)(2,1)}, bf16[128,2,1024]{2,1,0:T(2,128)(2,1)}) custom-call(s32[4]{0:T(128)} %bitcast.61, bf16[8,128,2,1024]{3,2,1,0:T(2,128)(2,1)} %kv_ref.7, bf16[8,5,256,128]{3,2,1,0:T(8,128)(2,1)} %bitcast.53), custom_call_target="tpu_custom_call" | custom-call | tf_op jit(solution)/shard_map/outgoing_pages/pallas_call | solution.py:90
  295.7 2.7 collective-permute-start.21
  302.0 6.3 %project.6 = (f32[64,4096]{1,0:T(8,128)}, bf16[64,4096]{1,0:T(8,128)(2,1)}, bf16[128,1024]{1,0:T(8,128)(2,1)}) custom-call(bf16[1072,128]{1,0:T(8,128)(2,1)} %copy-done.10, bf16[1072,128]{1,0:T(8,128)(2,1)} %copy-done.9, bf16[512,8192]{1,0:T(8,128)(2,1)} %refs_1_.3, bf16[512,8192]{1,0:T(8,128)(2,1)} %collective-permute-done.2.refs_3_.refs_2_), custom_call_target="tpu_custom_call" | custom-call | flops 1073741824 | bytes 8388608 | tf_op jit(solution)/shard_map/project/pallas_call | solution.py:482
  309.8 6.3 %project.4 = (f32[64,4096]{1,0:T(8,128)}, bf16[64,4096]{1,0:T(8,128)(2,1)}, bf16[128,1024]{1,0:T(8,128)(2,1)}) custom-call(bf16[1072,128]{1,0:T(8,128)(2,1)} %copy-done.12, bf16[1072,128]{1,0:T(8,128)(2,1)} %copy-done.11, bf16[512,8192]{1,0:T(8,128)(2,1)} %refs_1_.3, bf16[512,8192]{1,0:T(8,128)(2,1)} %collective-permute-done.2.refs_3_.refs_2_), custom_call_target="tpu_custom_call" | custom-call | flops 1073741824 | bytes 8388608 | tf_op jit(solution)/shard_map/project/pallas_call | solution.py:482
  316.1 6.2 %project.5 = (f32[64,4096]{1,0:T(8,128)}, bf16[64,4096]{1,0:T(8,128)(2,1)}) custom-call(bf16[128,1024]{1,0:T(8,128)(2,1)} %get-tuple-element.26.refs_0_, bf16[512,8192]{1,0:T(8,128)(2,1)} %refs_1_.3, bf16[512,8192]{1,0:T(8,128)(2,1)} %collective-permute-done.2.refs_3_.refs_2_), custom_call_target="tpu_custom_call" | custom-call | flops 1073741824 | bytes 8388608 | tf_op jit(solution)/shard_map/project/pallas_call | solution.py:482
  322.3 6.2 %project.7 = (f32[64,4096]{1,0:T(8,128)}, bf16[64,4096]{1,0:T(8,128)(2,1)}) custom-call(bf16[128,1024]{1,0:T(8,128)(2,1)} %get-tuple-element.31.refs_0_, bf16[512,8192]{1,0:T(8,128)(2,1)} %refs_1_.3, bf16[512,8192]{1,0:T(8,128)(2,1)} %collective-permute-done.2.refs_3_.refs_2_), custom_call_target="tpu_custom_call" | custom-call | flops 1073741824 | bytes 8388608 | tf_op jit(solution)/shard_map/project/pallas_call | solution.py:482
  333.6 113.2 %arrange_pages.1 = bf16[8,128,2,1024]{3,2,1,0:T(2,128)(2,1)} custom-call(s32[8]{0:T(128)} %page_after.1, s32[4]{0:T(128)} %bitcast.62, bf16[8,128,2,1024]{3,2,1,0:T(2,128)(2,1)} %kv_ref.7, bf16[128,2,1024]{2,1,0:T(2,128)(2,1)} %copy-done.5, bf16[128,2,1024]{2,1,0:T(2,128)(2,1)} %copy-done.6, bf16[128,2,1024]{2,1,0:T(2,128)(2,1)} %copy-done.7, ...), custom_call_target="tpu_custom_call" | custom-call | tf_op jit(solution)/shard_map/arrange_pages/pallas_call | solution.py:134
  448.2 17.8 %collective-permute-start.14 = (bf16[16,4096]{1,0:T(8,128)(2,1)S(1)}, bf16[16,4096]{1,0:T(8,128)(2,1)S(1)}, u32[]{:S(2)}, u32[]{:S(2)}) collective-permute-start(bf16[16,4096]{1,0:T(8,128)(2,1)S(1)} %get-tuple-element.64), channel_id=1, source_target_pairs={{0,4},{1,5},{2,6},{3,7},{4,0},{5,1},{6,2},{7,3},{8,12},{9,13},{10,... | collective-permute-start | bytes 393224 | tf_op jit(solution)/shard_map/ppermute | solution.py:32
  468.8 2.9 collective-permute-start.4
  475.7 2.9 collective-permute-start.8
  478.7 4.5 collective-permute-done.15
  484.9 2.8 collective-permute-start.18
  490.1 2.7 collective-permute-done.9
  494.5 3.9 collective-permute-done.19
  (120 shorter events, 49.2 us)
Async XLA Ops:
  91.0 63.0 %all-to-all-start.2 = ((bf16[8,5,128,2,128]{4,3,2,1,0:T(2,128)(2,1)}), bf16[8,5,128,2,128]{4,3,2,1,0:T(2,128)(2,1)S(1)}, u32[]{:S(2)}, u32[]{:S(2)}) async-start(bf16[8,5,128,2,128]{4,3,2,1,0:T(2,128)(2,1)} %split_heads.2), calls=%async_computation.2 | async-start | bytes 5242880 | tf_op jit(solution)/shard_map/all_to_all | solution.py:513
  94.7 206.3 %collective-permute-start.2 = (bf16[512,8192]{1,0:T(8,128)(2,1)}, bf16[512,8192]{1,0:T(8,128)(2,1)}, u32[]{:S(2)}, u32[]{:S(2)}) collective-permute-start(bf16[512,8192]{1,0:T(8,128)(2,1)} %refs_1_.3), channel_id=1, source_target_pairs={{0,1},{1,0},{2,3},{3,2},{4,5},{5,4},{6,7},{7,6},{8,9},{9,8},{10,11... | collective-permute-start | bytes 25165832 | tf_op jit(solution)/shard_map/ppermute | solution.py:32
  154.1 50.3 %all-to-all-start.1 = ((bf16[8,3,128,2,128]{4,3,2,1,0:T(2,128)(2,1)}), bf16[8,3,128,2,128]{4,3,2,1,0:T(2,128)(2,1)}, u32[]{:S(2)}, u32[]{:S(2)}) async-start(bf16[8,3,128,2,128]{4,3,2,1,0:T(2,128)(2,1)} %split_heads.3), calls=%async_computation.1 | async-start | bytes 3145728 | tf_op jit(solution)/shard_map/all_to_all | solution.py:513
  213.7 82.0 %collective-permute-start.12 = (bf16[1072,128]{1,0:T(8,128)(2,1)S(1)}, bf16[1072,128]{1,0:T(8,128)(2,1)S(1)}, u32[]{:S(2)}, u32[]{:S(2)}) collective-permute-start(bf16[1072,128]{1,0:T(8,128)(2,1)S(1)} %get-tuple-element.56), channel_id=1, source_target_pairs={{0,1},{1,9},{2,3},{3,11},{4,5},{5,13},{6,7},{7,15},{8,0},{9,8},{10... | collective-permute-start | bytes 823304 | tf_op jit(solution)/shard_map/ppermute | solution.py:32
  214.1 84.2 %collective-permute-start.11 = (bf16[1072,128]{1,0:T(8,128)(2,1)S(1)}, bf16[1072,128]{1,0:T(8,128)(2,1)S(1)}, u32[]{:S(2)}, u32[]{:S(2)}) collective-permute-start(bf16[1072,128]{1,0:T(8,128)(2,1)S(1)} %get-tuple-element.57), channel_id=1, source_target_pairs={{0,0},{1,8},{2,2},{3,10},{4,4},{5,12},{6,6},{7,14},{8,1},{9,9},{10... | collective-permute-start | bytes 823304 | tf_op jit(solution)/shard_map/ppermute | solution.py:32
  224.9 75.2 %collective-permute-start.1 = (bf16[1072,128]{1,0:T(8,128)(2,1)S(1)}, bf16[1072,128]{1,0:T(8,128)(2,1)S(1)}, u32[]{:S(2)}, u32[]{:S(2)}) collective-permute-start(bf16[1072,128]{1,0:T(8,128)(2,1)S(1)} %get-tuple-element.54), channel_id=1, source_target_pairs={{0,1},{1,9},{2,3},{3,11},{4,5},{5,13},{6,7},{7,15},{8,0},{9,8},{10... | collective-permute-start | bytes 823304 | tf_op jit(solution)/shard_map/ppermute | solution.py:32
  228.8 79.5 %collective-permute-start = (bf16[1072,128]{1,0:T(8,128)(2,1)}, bf16[1072,128]{1,0:T(8,128)(2,1)S(1)}, u32[]{:S(2)}, u32[]{:S(2)}) collective-permute-start(bf16[1072,128]{1,0:T(8,128)(2,1)} %get-tuple-element.55), channel_id=1, source_target_pairs={{0,0},{1,8},{2,2},{3,10},{4,4},{5,12},{6,6},{7,14},{8,1},{9,9},{10... | collective-permute-start | bytes 823304 | tf_op jit(solution)/shard_map/ppermute | solution.py:32
  295.7 32.8 %collective-permute-start.21 = (bf16[128,2,1024]{2,1,0:T(2,128)(2,1)}, bf16[128,2,1024]{2,1,0:T(2,128)(2,1)S(1)}, u32[]{:S(2)}, u32[]{:S(2)}) collective-permute-start(bf16[128,2,1024]{2,1,0:T(2,128)(2,1)} %get-tuple-element.34), channel_id=1, source_target_pairs={{0,1},{1,2},{2,3},{3,4},{4,5},{5,6},{6,7},{7,8},{8,9},{9,10},{10,1... | collective-permute-start | bytes 1572872 | tf_op jit(solution)/shard_map/ppermute | solution.py:32
  298.4 30.8 %collective-permute-start.22 = (bf16[128,2,1024]{2,1,0:T(2,128)(2,1)}, bf16[128,2,1024]{2,1,0:T(2,128)(2,1)S(1)}, u32[]{:S(2)}, u32[]{:S(2)}) collective-permute-start(bf16[128,2,1024]{2,1,0:T(2,128)(2,1)} %get-tuple-element.35), channel_id=1, source_target_pairs={{0,2},{1,3},{2,4},{3,5},{4,6},{5,7},{6,8},{7,9},{8,10},{9,11},{10,... | collective-permute-start | bytes 1572872 | tf_op jit(solution)/shard_map/ppermute | solution.py:32
  300.0 30.6 %collective-permute-start.23 = (bf16[128,2,1024]{2,1,0:T(2,128)(2,1)}, bf16[128,2,1024]{2,1,0:T(2,128)(2,1)S(1)}, u32[]{:S(2)}, u32[]{:S(2)}) collective-permute-start(bf16[128,2,1024]{2,1,0:T(2,128)(2,1)} %get-tuple-element.36), channel_id=1, source_target_pairs={{0,3},{1,4},{2,5},{3,6},{4,7},{5,8},{6,9},{7,10},{8,11},{9,12},{10... | collective-permute-start | bytes 1572872 | tf_op jit(solution)/shard_map/ppermute | solution.py:32
  300.9 31.9 %collective-permute-start.24 = (bf16[128,2,1024]{2,1,0:T(2,128)(2,1)}, bf16[128,2,1024]{2,1,0:T(2,128)(2,1)S(1)}, u32[]{:S(2)}, u32[]{:S(2)}) collective-permute-start(bf16[128,2,1024]{2,1,0:T(2,128)(2,1)} %get-tuple-element.37), channel_id=1, source_target_pairs={{0,4},{1,5},{2,6},{3,7},{4,8},{5,9},{6,10},{7,11},{8,12},{9,13},{1... | collective-permute-start | bytes 1572872 | tf_op jit(solution)/shard_map/ppermute | solution.py:32
  308.3 138.5 %collective-permute-start.13 = (bf16[64,4096]{1,0:T(8,128)(2,1)}, bf16[64,4096]{1,0:T(8,128)(2,1)}, u32[]{:S(2)}, u32[]{:S(2)}) collective-permute-start(bf16[64,4096]{1,0:T(8,128)(2,1)} %get-tuple-element.30), channel_id=1, source_target_pairs={{0,2},{1,3},{2,0},{3,1},{4,6},{5,7},{6,4},{7,5},{8,10},{9,11},{10,... | collective-permute-start | bytes 1572872 | tf_op jit(solution)/shard_map/ppermute | solution.py:32
  328.5 137.5 %collective-permute-start.3 = (bf16[64,4096]{1,0:T(8,128)(2,1)}, bf16[64,4096]{1,0:T(8,128)(2,1)}, u32[]{:S(2)}, u32[]{:S(2)}) collective-permute-start(bf16[64,4096]{1,0:T(8,128)(2,1)} %get-tuple-element.25), channel_id=1, source_target_pairs={{0,2},{1,3},{2,0},{3,1},{4,6},{5,7},{6,4},{7,5},{8,10},{9,11},{10,... | collective-permute-start | bytes 1572872 | tf_op jit(solution)/shard_map/ppermute | solution.py:32
  329.2 139.6 %collective-permute-start.7 = (bf16[64,4096]{1,0:T(8,128)(2,1)}, bf16[64,4096]{1,0:T(8,128)(2,1)}, u32[]{:S(2)}, u32[]{:S(2)}) collective-permute-start(bf16[64,4096]{1,0:T(8,128)(2,1)} %get-tuple-element.28), channel_id=1, source_target_pairs={{0,2},{1,3},{2,0},{3,1},{4,6},{5,7},{6,4},{7,5},{8,10},{9,11},{10,... | collective-permute-start | bytes 1572872 | tf_op jit(solution)/shard_map/ppermute | solution.py:32
  330.6 142.3 %collective-permute-start.17 = (bf16[64,4096]{1,0:T(8,128)(2,1)}, bf16[64,4096]{1,0:T(8,128)(2,1)}, u32[]{:S(2)}, u32[]{:S(2)}) collective-permute-start(bf16[64,4096]{1,0:T(8,128)(2,1)} %get-tuple-element.33.refs_4_), channel_id=1, source_target_pairs={{0,2},{1,3},{2,0},{3,1},{4,6},{5,7},{6,4},{7,5},{8,10},{9,11},{10,... | collective-permute-start | bytes 1572872 | tf_op jit(solution)/shard_map/ppermute | solution.py:32
  448.2 26.0 %collective-permute-start.14 = (bf16[16,4096]{1,0:T(8,128)(2,1)S(1)}, bf16[16,4096]{1,0:T(8,128)(2,1)S(1)}, u32[]{:S(2)}, u32[]{:S(2)}) collective-permute-start(bf16[16,4096]{1,0:T(8,128)(2,1)S(1)} %get-tuple-element.64), channel_id=1, source_target_pairs={{0,4},{1,5},{2,6},{3,7},{4,0},{5,1},{6,2},{7,3},{8,12},{9,13},{10,... | collective-permute-start | bytes 393224 | tf_op jit(solution)/shard_map/ppermute | solution.py:32
  466.0 9.7 %collective-permute-start.16 = (bf16[16,4096]{1,0:T(8,128)(2,1)S(1)}, bf16[16,4096]{1,0:T(8,128)(2,1)S(1)}, u32[]{:S(2)}, u32[]{:S(2)}) collective-permute-start(bf16[16,4096]{1,0:T(8,128)(2,1)S(1)} %get-tuple-element.65), channel_id=1, source_target_pairs={{0,12},{1,13},{2,14},{3,15},{4,8},{5,9},{6,10},{7,11},{8,4},{9,5},... | collective-permute-start | bytes 393224 | tf_op jit(solution)/shard_map/ppermute | solution.py:32
  466.0 17.1 %collective-permute-start.15 = (bf16[16,4096]{1,0:T(8,128)(2,1)S(1)}, bf16[16,4096]{1,0:T(8,128)(2,1)S(1)}, u32[]{:S(2)}, u32[]{:S(2)}) collective-permute-start(bf16[16,4096]{1,0:T(8,128)(2,1)S(1)} %get-tuple-element.66), channel_id=1, source_target_pairs={{0,8},{1,9},{2,10},{3,11},{4,12},{5,13},{6,14},{7,15},{8,0},{9,1},... | collective-permute-start | bytes 393224 | tf_op jit(solution)/shard_map/ppermute | solution.py:32
  468.8 16.0 %collective-permute-start.4 = (bf16[16,4096]{1,0:T(8,128)(2,1)S(1)}, bf16[16,4096]{1,0:T(8,128)(2,1)S(1)}, u32[]{:S(2)}, u32[]{:S(2)}) collective-permute-start(bf16[16,4096]{1,0:T(8,128)(2,1)S(1)} %get-tuple-element.58), channel_id=1, source_target_pairs={{0,4},{1,5},{2,6},{3,7},{4,0},{5,1},{6,2},{7,3},{8,12},{9,13},{10,... | collective-permute-start | bytes 393224 | tf_op jit(solution)/shard_map/ppermute | solution.py:32
  472.9 12.0 %collective-permute-start.6 = (bf16[16,4096]{1,0:T(8,128)(2,1)S(1)}, bf16[16,4096]{1,0:T(8,128)(2,1)S(1)}, u32[]{:S(2)}, u32[]{:S(2)}) collective-permute-start(bf16[16,4096]{1,0:T(8,128)(2,1)S(1)} %get-tuple-element.59), channel_id=1, source_target_pairs={{0,12},{1,13},{2,14},{3,15},{4,8},{5,9},{6,10},{7,11},{8,4},{9,5},... | collective-permute-start | bytes 393224 | tf_op jit(solution)/shard_map/ppermute | solution.py:32
  474.2 13.4 %collective-permute-start.5 = (bf16[16,4096]{1,0:T(8,128)(2,1)S(1)}, bf16[16,4096]{1,0:T(8,128)(2,1)S(1)}, u32[]{:S(2)}, u32[]{:S(2)}) collective-permute-start(bf16[16,4096]{1,0:T(8,128)(2,1)S(1)} %get-tuple-element.60), channel_id=1, source_target_pairs={{0,8},{1,9},{2,10},{3,11},{4,12},{5,13},{6,14},{7,15},{8,0},{9,1},... | collective-permute-start | bytes 393224 | tf_op jit(solution)/shard_map/ppermute | solution.py:32
  475.7 13.9 %collective-permute-start.8 = (bf16[16,4096]{1,0:T(8,128)(2,1)S(1)}, bf16[16,4096]{1,0:T(8,128)(2,1)S(1)}, u32[]{:S(2)}, u32[]{:S(2)}) collective-permute-start(bf16[16,4096]{1,0:T(8,128)(2,1)S(1)} %get-tuple-element.61), channel_id=1, source_target_pairs={{0,4},{1,5},{2,6},{3,7},{4,0},{5,1},{6,2},{7,3},{8,12},{9,13},{10,... | collective-permute-start | bytes 393224 | tf_op jit(solution)/shard_map/ppermute | solution.py:32
  484.9 8.0 %collective-permute-start.18 = (bf16[16,4096]{1,0:T(8,128)(2,1)S(1)}, bf16[16,4096]{1,0:T(8,128)(2,1)S(1)}, u32[]{:S(2)}, u32[]{:S(2)}) collective-permute-start(bf16[16,4096]{1,0:T(8,128)(2,1)S(1)} %get-tuple-element.67), channel_id=1, source_target_pairs={{0,4},{1,5},{2,6},{3,7},{4,0},{5,1},{6,2},{7,3},{8,12},{9,13},{10,... | collective-permute-start | bytes 393224 | tf_op jit(solution)/shard_map/ppermute | solution.py:32
  489.7 8.7 %collective-permute-start.19 = (bf16[16,4096]{1,0:T(8,128)(2,1)S(1)}, bf16[16,4096]{1,0:T(8,128)(2,1)S(1)}, u32[]{:S(2)}, u32[]{:S(2)}) collective-permute-start(bf16[16,4096]{1,0:T(8,128)(2,1)S(1)} %get-tuple-element.69), channel_id=1, source_target_pairs={{0,8},{1,9},{2,10},{3,11},{4,12},{5,13},{6,14},{7,15},{8,0},{9,1},... | collective-permute-start | bytes 393224 | tf_op jit(solution)/shard_map/ppermute | solution.py:32
  (18 other events, 335.0 us)

commit v3 on v2

--- a/solution.py
+++ b/solution.py
@@ -10,7 +10,6 @@
 HEADS = 64
 KV_HEADS = 8
 HEAD_DIM = 128
-D = 8192
 PAGE_TOK = 128
 BLOCK = 256
 MOVE_WIN = 4
@@ -37,52 +36,64 @@
     return (j % 2) * half + j // 2
 
 
-def split_heads_kernel(kv_ref, out_ref, sems, *, first):
-    copies = []
-    for d in range(KV_HEADS):
-        copies.append(
-            pltpu.make_async_copy(
-                kv_ref.at[
-                    pl.ds(first, out_ref.shape[1]),
-                    :,
-                    :,
-                    pl.ds(head_of(d) * HEAD_DIM, HEAD_DIM),
-                ],
-                out_ref.at[d],
-                sems.at[d],
-            )
+def split_heads_kernel(kv_ref, out_ref, buf, in_sems, out_sems, *, first):
+    count = out_ref.shape[1]
+    loads = [
+        pltpu.make_async_copy(
+            kv_ref.at[pl.ds(first, count), :, :, pl.ds(head_of(d) * HEAD_DIM, HEAD_DIM)],
+            buf.at[d],
+            in_sems.at[d],
         )
-    for copy in copies:
-        copy.start()
-    for copy in copies:
-        copy.wait()
+        for d in range(KV_HEADS)
+    ]
+    stores = [
+        pltpu.make_async_copy(buf.at[d], out_ref.at[d], out_sems.at[d])
+        for d in range(KV_HEADS)
+    ]
+    for load in loads:
+        load.start()
+    for load, store in zip(loads, stores):
+        load.wait()
+        store.start()
+    for store in stores:
+        store.wait()
 
 
 def split_heads(kv_cache, first, count):
+    shape = (KV_HEADS, count, PAGE_TOK, 2, HEAD_DIM)
     return pl.pallas_call(
         functools.partial(split_heads_kernel, first=first),
-        out_shape=jax.ShapeDtypeStruct(
-            (KV_HEADS, count, PAGE_TOK, 2, HEAD_DIM), kv_cache.dtype
-        ),
+        out_shape=jax.ShapeDtypeStruct(shape, kv_cache.dtype),
         in_specs=[ANY],
         out_specs=ANY,
-        scratch_shapes=[pltpu.SemaphoreType.DMA((KV_HEADS,))],
+        scratch_shapes=[
+            pltpu.VMEM(shape, kv_cache.dtype),
+            pltpu.SemaphoreType.DMA((KV_HEADS,)),
+            pltpu.SemaphoreType.DMA((KV_HEADS,)),
+        ],
         name="split_heads",
     )(kv_cache)
 
 
 def outgoing_kernel(move_out, kv_ref, after_ref, *refs):
-    outs, sems = refs[:MOVE_WIN], refs[MOVE_WIN]
-    copies = [
+    outs = refs[:MOVE_WIN]
+    buf, in_sems, out_sems = refs[MOVE_WIN:]
+    loads = [
         pltpu.make_async_copy(
-            kv_ref.at[jnp.maximum(move_out[o], 0)], outs[o], sems.at[o]
+            kv_ref.at[jnp.maximum(move_out[o], 0)], buf.at[o], in_sems.at[o]
         )
         for o in range(MOVE_WIN)
     ]
-    for copy in copies:
-        copy.start()
-    for copy in copies:
-        copy.wait()
+    stores = [
+        pltpu.make_async_copy(buf.at[o], outs[o], out_sems.at[o]) for o in range(MOVE_WIN)
+    ]
+    for load in loads:
+        load.start()
+    for load, store in zip(loads, stores):
+        load.wait()
+        store.start()
+    for store in stores:
+        store.wait()
 
 
 def outgoing_pages(kv_cache, move_out, after):
@@ -95,7 +106,11 @@
             grid=(),
             in_specs=[ANY, ANY],
             out_specs=(ANY,) * MOVE_WIN,
-            scratch_shapes=[pltpu.SemaphoreType.DMA((MOVE_WIN,))],
+            scratch_shapes=[
+                pltpu.VMEM((MOVE_WIN,) + kv_cache.shape[1:], kv_cache.dtype),
+                pltpu.SemaphoreType.DMA((MOVE_WIN,)),
+                pltpu.SemaphoreType.DMA((MOVE_WIN,)),
+            ],
         ),
         name="outgoing_pages",
     )(move_out, kv_cache, after)
@@ -103,9 +118,9 @@
 
 def arrange_kernel(page_after, move_in, kv_ref, *refs):
     arrived = refs[:MOVE_WIN]
-    _, out_ref, zero_ref, sems = refs[MOVE_WIN:]
-    zero_ref[...] = jnp.zeros(zero_ref.shape, zero_ref.dtype)
+    _, out_ref, buf, zero_ref, in_sems, out_sems = refs[MOVE_WIN:]
     slots = out_ref.shape[0]
+    filled = []
     for s in range(slots):
         taken = jnp.zeros((), jnp.bool_)
         for o in reversed(range(MOVE_WIN)):
@@ -113,24 +128,34 @@
 
             @pl.when(lands & jnp.logical_not(taken))
             def _():
-                pltpu.make_async_copy(arrived[o], out_ref.at[s], sems.at[s]).start()
+                pltpu.make_async_copy(arrived[o], buf.at[s], in_sems.at[s]).start()
 
             taken = taken | lands
         kept = page_after[s] >= 0
 
         @pl.when(kept & jnp.logical_not(taken))
         def _():
-            pltpu.make_async_copy(kv_ref.at[s], out_ref.at[s], sems.at[s]).start()
-
-        @pl.when(jnp.logical_not(kept | taken))
+            pltpu.make_async_copy(kv_ref.at[s], buf.at[s], in_sems.at[s]).start()
+
+        filled.append(kept | taken)
+    zero_ref[...] = jnp.zeros(zero_ref.shape, zero_ref.dtype)
+    for s in range(slots):
+
+        @pl.when(filled[s])
         def _():
-            pltpu.make_async_copy(zero_ref, out_ref.at[s], sems.at[s]).start()
+            pltpu.make_async_copy(kv_ref.at[s], buf.at[s], in_sems.at[s]).wait()
+            pltpu.make_async_copy(buf.at[s], out_ref.at[s], out_sems.at[s]).start()
+
+        @pl.when(jnp.logical_not(filled[s]))
+        def _():
+            pltpu.make_async_copy(zero_ref, out_ref.at[s], out_sems.at[s]).start()
 
     for s in range(slots):
-        pltpu.make_async_copy(kv_ref.at[s], out_ref.at[s], sems.at[s]).wait()
+        pltpu.make_async_copy(zero_ref, out_ref.at[s], out_sems.at[s]).wait()
 
 
 def arrange_pages(kv_cache, arrived, page_after, move_in, after):
+    slots = kv_cache.shape[0]
     return pl.pallas_call(
         arrange_kernel,
         out_shape=jax.ShapeDtypeStruct(kv_cache.shape, kv_cache.dtype),
@@ -140,12 +165,53 @@
             in_specs=[ANY] * (2 + MOVE_WIN),
             out_specs=ANY,
             scratch_shapes=[
+                pltpu.VMEM(kv_cache.shape, kv_cache.dtype),
                 pltpu.VMEM(kv_cache.shape[1:], kv_cache.dtype),
-                pltpu.SemaphoreType.DMA((kv_cache.shape[0],)),
+                pltpu.SemaphoreType.DMA((slots,)),
+                pltpu.SemaphoreType.DMA((slots,)),
             ],
         ),
         name="arrange_pages",
     )(page_after, move_in, kv_cache, *arrived, after)
+
+
+def rows_kernel(place, q_ref, out_ref, *, ways, tok_rows):
+    tok = out_ref.shape[1] // GROUP
+    gp = GROUP // ways
+    head = place[0]
+    t_rel = pl.program_id(0) // 2
+    t = place[1] ^ t_rel
+    for p in range(KV_HEADS):
+        kx = (p % (KV_HEADS // 2)) * 2 + p // (KV_HEADS // 2)
+        at = pl.multiple_of(((kx ^ head) * ways + t) * tok_rows, tok_rows)
+        for gx in range(GROUP):
+            g = ((gx // gp) ^ t) * gp + gx % gp
+            lanes = pl.ds(pl.multiple_of(g * HEAD_DIM, HEAD_DIM), HEAD_DIM)
+            to = gx * tok + p * tok_rows
+            out_ref[0, to : to + tok_rows, :] = q_ref[0, pl.ds(at, tok_rows), lanes]
+
+
+def query_rows(queries, place, ways, tok_rows):
+    width = GROUP * HEAD_DIM
+    tok = KV_HEADS * tok_rows
+    dtype = queries.dtype
+    if tok_rows % 16:
+        queries = lax.dynamic_slice_in_dim(queries, place[0] * width, width, axis=2)
+        queries = queries.astype(jnp.float32)
+        column = lambda i, place: (i % 2, 0, 0)
+    else:
+        column = lambda i, place: (i % 2, 0, place[0])
+    return pl.pallas_call(
+        functools.partial(rows_kernel, ways=ways, tok_rows=tok_rows),
+        out_shape=jax.ShapeDtypeStruct((2 * ways, GROUP * tok, HEAD_DIM), queries.dtype),
+        grid_spec=pltpu.PrefetchScalarGridSpec(
+            num_scalar_prefetch=1,
+            grid=(2 * ways,),
+            in_specs=[pl.BlockSpec((1, queries.shape[1], width), column)],
+            out_specs=pl.BlockSpec((1, GROUP * tok, HEAD_DIM), lambda i, place: (i, 0, 0)),
+        ),
+        name="query_rows",
+    )(place, queries).astype(dtype)
 
 
 def three_parts(x):
@@ -157,7 +223,7 @@
 
 
 def attend_kernel(
-    pages, place, x_ref, q_ref, *refs, first, last, rows, tok, ways, tok_rows, block
+    pages, place, x_ref, q_ref, after_ref, *refs, first, last, rows, tok, ways, tok_rows, block
 ):
     n_in = 0 if first else 2
     carried = refs[:n_in]
@@ -338,14 +404,13 @@
             out_ref[0, at : at + 2 * GROUP, :] = piece
 
 
-def attend(pages, place, x, q, carried, block, tok_rows, rows):
+def attend(pages, place, x, q, after, carried, block, tok_rows, rows):
     sources, src_slots = x.shape[:2]
     steps, total, _ = q.shape
     tok = total // GROUP
     first = carried is None
     last = block is not None
     ways = steps // 2
-    pad = WIDE - 1
     n_slots = -(-sources * src_slots // WIDE) * WIDE
     if last:
         grid = ways
@@ -357,6 +422,7 @@
     in_specs = [
         pl.BlockSpec(x.shape, lambda i, *_: (0, 0, 0, 0)),
         pl.BlockSpec((1, total, HEAD_DIM), at),
+        ANY,
     ]
     sent = total + 3 * 2 * GROUP
     if last:
@@ -409,7 +475,7 @@
             flops=flops, transcendentals=flops // (8 * HEAD_DIM), bytes_accessed=x.size * 2
         ),
         name="attend_last" if last else "attend_first",
-    )(pages, place, x, q, *extra)
+    )(pages, place, x, q, after, *extra)
 
 
 def merge(parts, a_ref, tok):
@@ -503,7 +569,6 @@
     ways = n // KV_HEADS
     tok_rows = BLOCK // n
     tok = BLOCK // ways
-    gp = GROUP // ways
     me = lax.axis_index("pages")
     way = me // KV_HEADS
     head = head_of(me % KV_HEADS)
@@ -513,69 +578,70 @@
         return lax.all_to_all(x, "pages", 0, 0, axis_index_groups=groups, tiled=True)
 
     cuts = [(0, FIRST_SLOTS), (FIRST_SLOTS, slots - FIRST_SLOTS)]
-    pieces = [split_heads(kv_cache, at, count) for at, count in cuts]
-    arrived = [
-        exchange(piece).reshape(KV_HEADS, count, 2 * PAGE_TOK, HEAD_DIM)
-        for piece, (_, count) in zip(pieces, cuts)
-    ]
-    table_in, _ = lax.optimization_barrier((slot_page_before, pieces[0]))
-    table = exchange(jnp.broadcast_to(table_in[None, None], (KV_HEADS, 1, slots)))
+    arrived = []
+    for at, count in cuts:
+        piece = split_heads(kv_cache, at, count)
+        got = exchange(piece)
+        arrived.append(got.reshape(KV_HEADS, count, 2 * PAGE_TOK, HEAD_DIM))
+    table = exchange(jnp.broadcast_to(slot_page_before[None, None], (KV_HEADS, 1, slots)))
     table = table.reshape(KV_HEADS, slots)
+    pages = [table[:, at : at + count].reshape(-1) for at, count in cuts]
     place = jnp.stack([head, way, positions[0, 0], positions[1, 0]]).astype(jnp.int32)
-
-    xs = lambda m: jnp.arange(m, dtype=jnp.int32)
-    t_of = way ^ xs(ways)
-    kx = (xs(KV_HEADS) % (KV_HEADS // 2)) * 2 + xs(KV_HEADS) // (KV_HEADS // 2)
-    owner = (kx[None, :] ^ head) * ways + t_of[:, None]
-    g_of = ((xs(GROUP) // gp)[None, :] ^ t_of[:, None]) * gp + (xs(GROUP) % gp)[None, :]
-    mine = lax.dynamic_slice_in_dim(queries, head * GROUP * HEAD_DIM, GROUP * HEAD_DIM, axis=2)
-    mine = mine.reshape(2, n, tok_rows, GROUP, HEAD_DIM)
-    q_rows = []
-    for tx in range(ways):
-        taken = jnp.take(jnp.take(mine, owner[tx], axis=1), g_of[tx], axis=3)
-        q_rows.append(jnp.transpose(taken, (0, 3, 1, 2, 4)).reshape(2, GROUP * tok, HEAD_DIM))
-    q = jnp.concatenate(q_rows, axis=0)
+    q = query_rows(queries, place, ways, tok_rows)
+
+    leaving = outgoing_pages(kv_cache, move_out[0], arrived[0])
+    landed = []
+    for o in range(1, MOVE_WIN + 1):
+        landed.append(permute_to(leaving[o - 1], n, lambda i: (i + o) % n))
+
+    ws = [w_out]
+    for s in range(1, ways):
+        ws.append(permute_to(w_out, n, lambda i: i ^ s))
 
     rows = 2 * tok
-    pages = [table[:, at : at + count].reshape(-1) for at, count in cuts]
-    carried = attend(pages[0], place, arrived[0], q, None, None, tok_rows, rows)
-
-    leaving = outgoing_pages(kv_cache, move_out[0], arrived[0])
-    landed = [
-        permute_to(leaving[o - 1], n, lambda i: (i + o) % n) for o in range(1, MOVE_WIN + 1)
-    ]
-
-    ws = [w_out] + [permute_to(w_out, n, lambda i: i ^ s) for s in range(1, ways)]
+    carried = attend(pages[0], place, arrived[0], q, leaving[0], None, None, tok_rows, rows)
 
     def merger(i, s):
         return head_of(i % KV_HEADS) * ways + ((i // KV_HEADS) ^ s)
 
     partial = []
     for b in range(2):
-        (out,) = attend(pages[1], place, arrived[1], q, carried, b, tok_rows, rows)
-        partial.append([permute_to(out[s], n, lambda i: merger(i, s)) for s in range(ways)])
-
-    results = []
+        (out,) = attend(
+            pages[1], place, arrived[1], q, leaving[0], carried, b, tok_rows, rows
+        )
+        parts = []
+        for s in range(ways):
+            parts.append(permute_to(out[s], n, lambda i: merger(i, s)))
+        partial.append(parts)
+
+    sums = []
     for b in range(2):
         merged = partial[b]
-        columns = []
         for c in range(COLUMN_PARTS):
             keep, send, *a = project(merged, ws, tok, c)
             if a:
                 merged = a
             got = permute_to(send, n, lambda i: i ^ ways)
-            total = (keep + got.astype(jnp.float32)).reshape(KV_HEADS // 2, tok_rows, -1)
-            mine_rows = total[0]
-            for zx in range(1, KV_HEADS // 2):
-                got = permute_to(
-                    total[zx].astype(jnp.bfloat16), n, lambda i: i ^ (zx * 2 * ways)
-                )
-                mine_rows = mine_rows + got.astype(jnp.float32)
-            columns.append(mine_rows.astype(jnp.bfloat16))
-        results.append(jnp.concatenate(columns, axis=1))
-
+            sums.append((keep, got))
     cache_after = arrange_pages(kv_cache, landed, slot_page_after, move_in[0], send)
-    return (jnp.stack(results), cache_after)
+
+    results = []
+    for keep, got in sums:
+        total = (keep + got.astype(jnp.float32)).reshape(KV_HEADS // 2, tok_rows, -1)
+        mine_rows = total[0]
+        for zx in range(1, KV_HEADS // 2):
+            got = permute_to(
+                total[zx].astype(jnp.bfloat16), n, lambda i: i ^ (zx * 2 * ways)
+            )
+            mine_rows = mine_rows + got.astype(jnp.float32)
+        results.append(mine_rows.astype(jnp.bfloat16))
+    out = jnp.stack(
+        [
+            jnp.concatenate(results[b * COLUMN_PARTS : (b + 1) * COLUMN_PARTS], axis=1)
+            for b in range(2)
+        ]
+    )
+    return (out, cache_after)
 
 
 def solution(mesh):

time: 508 us -> 257 us (0.51); the launches traced: 499 us -> 256 us
  Pallas kernels: 385 us -> 93.1 us
  waiting for transfers between devices: 13.1 us -> 80.7 us
  local copies, waits for them, and re-layouts: 17.9 us -> 6.9 us
  blocking collectives: 9.76 us -> 0 us
  starting transfers between devices: 60.2 us -> 66.8 us
    pallas_call x2, Pallas kernels: 129 us -> 4.9 us  [split_heads(): pl.pallas_call(functools.partial(split_heads_kernel, first=first), out_sh...]
    pallas_call x1, Pallas kernels: 113 us -> 4.02 us  [arrange_pages(): pl.pallas_call(arrange_kernel, out_shape=jax.ShapeDtypeStruct(kv_cache.sh...]
    pallas_call x1, Pallas kernels: 65.3 us -> 3.11 us  [outgoing_pages(): pl.pallas_call(outgoing_kernel, out_shape=(page,) * MOVE_WIN, grid_spec=p...]
    ppermute x25, waiting for transfers between devices: 13.1 us -> 50.2 us  [permute_to(): return lax.ppermute(x, 'pages', [(i, target(i)) for i in range(n)])]
    all_to_all x2 -> x3, waiting for transfers between devices: 0.01 us -> 30.5 us  [exchange(): lax.all_to_all(x, 'pages', 0, 0, axis_index_groups=groups, tiled=True)]
    all_to_all x1 -> x0, blocking collectives: 9.76 us -> none  [exchange(): lax.all_to_all(x, 'pages', 0, 0, axis_index_groups=groups, tiled=True)]
    gather x4 -> x0, local copies, waits for them, and re-layouts: 7.69 us -> none  [local(): taken = jnp.take(jnp.take(mine, owner[tx], axis=1), g_of[tx], axis=3)]
    all_to_all x2 -> x3, starting transfers between devices: 7.94 us -> 13.2 us  [exchange(): lax.all_to_all(x, 'pages', 0, 0, axis_index_groups=groups, tiled=True)]
  transfers between devices with their start and end apart: 27 -> 28, of which waited for: 5 -> 9; matrix products, arithmetic and copies ran while one was open for 6% -> 5% of each run, Pallas kernels for 61% -> 36%
where the time goes in v3:
time: 257 us; the launch traced here: 256 us
  Pallas kernels  93.1 us (36%)
  waiting for transfers between devices  80.7 us (31%)
  starting transfers between devices  66.8 us (26%)
  other arithmetic  7.85 us (3%)
  local copies, waits for them, and re-layouts  6.9 us (3%)
    ppermute x25, starting transfers between devices, permute_to(): return lax.ppermute(x, 'pages', [(i, target(i)) for i in range(n)])  53.6 us
    pallas_call x3, Pallas kernels, attend(): pl.pallas_call(functools.partial(attend_kernel, first=first, last=last, r...  51.7 us
    ppermute x25, waiting for transfers between devices, permute_to(): return lax.ppermute(x, 'pages', [(i, target(i)) for i in range(n)])  50.2 us
    all_to_all x3, waiting for transfers between devices, exchange(): lax.all_to_all(x, 'pages', 0, 0, axis_index_groups=groups, tiled=True)  30.5 us
    pallas_call x4, Pallas kernels, project(): pl.pallas_call(functools.partial(project_kernel, n_parts=len(parts), n_ws...  24.9 us
    all_to_all x3, starting transfers between devices, exchange(): lax.all_to_all(x, 'pages', 0, 0, axis_index_groups=groups, tiled=True)  13.2 us
  transfers between devices with their start and end apart: 28, of which 9 were waited for; matrix products, arithmetic and copies ran while one was open for 5% of the time, Pallas kernels for 36%

profile of v3, /device:TPU:0, one launch (start us, length us, event | category | flops | bytes accessed | tf_op | source)
XLA Modules:
  0.0 256.4 jit_solution(16671788506428663914)
XLA Ops:
  1.9 5.3 %all-to-all-start = ((s32[8,1,8]{2,1,0:T(1,128)}), s32[8,1,8]{2,1,0:T(1,128)S(1)}, u32[]{:S(2)}, u32[]{:S(2)}) async-start(s32[8,1,8]{2,1,0:T(1,128)} %broadcast_in_dim.2), calls=%async_computation | async-start | bytes 8192 | tf_op jit(solution)/shard_map/all_to_all | solution.py:578
  11.8 3.6 %all-to-all-start.2 = ((bf16[8,5,128,2,128]{4,3,2,1,0:T(2,128)(2,1)}), bf16[8,5,128,2,128]{4,3,2,1,0:T(2,128)(2,1)S(1)}, u32[]{:S(2)}, u32[]{:S(2)}) async-start(bf16[8,5,128,2,128]{4,3,2,1,0:T(2,128)(2,1)} %split_heads.3), calls=%async_computation.2 | async-start | bytes 5242880 | tf_op jit(solution)/shard_map/all_to_all | solution.py:578
  18.1 28.5 %all-to-all-done.2 = bf16[8,5,128,2,128]{4,3,2,1,0:T(2,128)(2,1)S(1)} async-done(((bf16[8,5,128,2,128]{4,3,2,1,0:T(2,128)(2,1)}), bf16[8,5,128,2,128]{4,3,2,1,0:T(2,128)(2,1)S(1)}, u32[]{:S(2)}, u32[]{:S(2)}) %all-to-all-start.2) | async-done | bytes 2621472 | tf_op jit(solution)/shard_map/all_to_all | solution.py:578
  46.7 4.3 %all-to-all-start.1 = ((bf16[8,3,128,2,128]{4,3,2,1,0:T(2,128)(2,1)}), bf16[8,3,128,2,128]{4,3,2,1,0:T(2,128)(2,1)}, u32[]{:S(2)}, u32[]{:S(2)}) async-start(bf16[8,3,128,2,128]{4,3,2,1,0:T(2,128)(2,1)} %split_heads.2), calls=%async_computation.1 | async-start | bytes 3145728 | tf_op jit(solution)/shard_map/all_to_all | solution.py:578
  53.5 4.4 %query_rows.1.q_ref = bf16[4,1024,128]{2,1,0:T(8,128)(2,1)} custom-call(s32[4]{0:T(128)} %pad_add_fusion.place, bf16[2,256,8192]{2,1,0:T(8,128)(2,1)} %q_ref.1), custom_call_target="tpu_custom_call" | custom-call | tf_op jit(solution)/shard_map/query_rows/pallas_call | solution.py:204
  62.3 35.2 %attend_first.1 = (f32[4,1024,256]{2,1,0:T(8,128)}, f32[4,1024,128]{2,1,0:T(8,128)}) custom-call(s32[40]{0:T(128)} %reshape.62.pages, s32[4]{0:T(128)} %pad_add_fusion.place, bf16[8,5,256,128]{3,2,1,0:T(8,128)(2,1)} %bitcast.23, bf16[4,1024,128]{2,1,0:T(8,128)(2,1)} %query_rows.1.q_ref, bf16[128,2,1024]{2,1,0:T(2,128)(2,1)} %get-tuple-element.18.after_ref), custom_call_target="tpu_custom_call" | custom-call | flops 21474836480 | bytes 2621440 | tf_op jit(solution)/shard_map/attend_first/pallas_call | solution.py:448
  97.5 8.2 %attend_last.3 = bf16[2,1072,128]{2,1,0:T(8,128)(2,1)} custom-call(s32[24]{0:T(128)} %reshape.59.pages, s32[4]{0:T(128)} %pad_add_fusion.place, bf16[8,3,256,128]{3,2,1,0:T(8,128)(2,1)} %bitcast.5.x_ref, bf16[4,1024,128]{2,1,0:T(8,128)(2,1)} %query_rows.1.q_ref, bf16[128,2,1024]{2,1,0:T(2,128)(2,1)} %get-tuple-element.18.after_ref, ...), custom_call_target="tpu_custom_call" | custom-call | flops 6442450944 | bytes 1572864 | tf_op jit(solution)/shard_map/attend_last/pallas_call | solution.py:448
  107.9 8.3 %attend_last.2 = bf16[2,1072,128]{2,1,0:T(8,128)(2,1)} custom-call(s32[24]{0:T(128)} %reshape.59.pages, s32[4]{0:T(128)} %pad_add_fusion.place, bf16[8,3,256,128]{3,2,1,0:T(8,128)(2,1)} %bitcast.5.x_ref, bf16[4,1024,128]{2,1,0:T(8,128)(2,1)} %query_rows.1.q_ref, bf16[128,2,1024]{2,1,0:T(2,128)(2,1)} %get-tuple-element.18.after_ref, ...), custom_call_target="tpu_custom_call" | custom-call | flops 6442450944 | bytes 1572864 | tf_op jit(solution)/shard_map/attend_last/pallas_call | solution.py:448
  117.9 3.9 %collective-permute-start.1 = (bf16[1072,128]{1,0:T(8,128)(2,1)S(1)}, bf16[1072,128]{1,0:T(8,128)(2,1)S(1)}, u32[]{:S(2)}, u32[]{:S(2)}) collective-permute-start(bf16[1072,128]{1,0:T(8,128)(2,1)S(1)} %get-tuple-element.42), channel_id=1, source_target_pairs={{0,1},{1,9},{2,3},{3,11},{4,5},{5,13},{6,7},{7,15},{8,0},{9,8},{10... | collective-permute-start | bytes 823304 | tf_op jit(solution)/shard_map/ppermute | solution.py:31
  127.7 6.6 %collective-permute-done.1.refs_1_ = bf16[1072,128]{1,0:T(8,128)(2,1)S(1)} collective-permute-done((bf16[1072,128]{1,0:T(8,128)(2,1)S(1)}, bf16[1072,128]{1,0:T(8,128)(2,1)S(1)}, u32[]{:S(2)}, u32[]{:S(2)}) %collective-permute-start.1) | collective-permute-done | bytes 274464 | tf_op jit(solution)/shard_map/ppermute | solution.py:31
  135.8 6.3 %project.6 = (f32[64,4096]{1,0:T(8,128)}, bf16[64,4096]{1,0:T(8,128)(2,1)}, bf16[128,1024]{1,0:T(8,128)(2,1)}) custom-call(bf16[1072,128]{1,0:T(8,128)(2,1)} %copy-done.10, bf16[1072,128]{1,0:T(8,128)(2,1)} %copy-done.9, bf16[512,8192]{1,0:T(8,128)(2,1)} %refs_1_.3, bf16[512,8192]{1,0:T(8,128)(2,1)} %collective-permute-done.2.refs_3_.refs_2_), custom_call_target="tpu_custom_call" | custom-call | flops 1073741824 | bytes 8388608 | tf_op jit(solution)/shard_map/project/pallas_call | solution.py:548
  142.1 22.8 %collective-permute-start.13 = (bf16[64,4096]{1,0:T(8,128)(2,1)}, bf16[64,4096]{1,0:T(8,128)(2,1)}, u32[]{:S(2)}, u32[]{:S(2)}) collective-permute-start(bf16[64,4096]{1,0:T(8,128)(2,1)} %get-tuple-element.27), channel_id=1, source_target_pairs={{0,2},{1,3},{2,0},{3,1},{4,6},{5,7},{6,4},{7,5},{8,10},{9,11},{10,... | collective-permute-start | bytes 1572872 | tf_op jit(solution)/shard_map/ppermute | solution.py:31
  165.0 6.3 %project.4 = (f32[64,4096]{1,0:T(8,128)}, bf16[64,4096]{1,0:T(8,128)(2,1)}, bf16[128,1024]{1,0:T(8,128)(2,1)}) custom-call(bf16[1072,128]{1,0:T(8,128)(2,1)} %copy-done.12, bf16[1072,128]{1,0:T(8,128)(2,1)} %copy-done.11, bf16[512,8192]{1,0:T(8,128)(2,1)} %refs_1_.3, bf16[512,8192]{1,0:T(8,128)(2,1)} %collective-permute-done.2.refs_3_.refs_2_), custom_call_target="tpu_custom_call" | custom-call | flops 1073741824 | bytes 8388608 | tf_op jit(solution)/shard_map/project/pallas_call | solution.py:548
  171.2 6.2 %project.5 = (f32[64,4096]{1,0:T(8,128)}, bf16[64,4096]{1,0:T(8,128)(2,1)}) custom-call(bf16[128,1024]{1,0:T(8,128)(2,1)} %get-tuple-element.23.refs_0_, bf16[512,8192]{1,0:T(8,128)(2,1)} %refs_1_.3, bf16[512,8192]{1,0:T(8,128)(2,1)} %collective-permute-done.2.refs_3_.refs_2_), custom_call_target="tpu_custom_call" | custom-call | flops 1073741824 | bytes 8388608 | tf_op jit(solution)/shard_map/project/pallas_call | solution.py:548
  177.4 6.2 %project.7 = (f32[64,4096]{1,0:T(8,128)}, bf16[64,4096]{1,0:T(8,128)(2,1)}) custom-call(bf16[128,1024]{1,0:T(8,128)(2,1)} %get-tuple-element.28.refs_0_, bf16[512,8192]{1,0:T(8,128)(2,1)} %refs_1_.3, bf16[512,8192]{1,0:T(8,128)(2,1)} %collective-permute-done.2.refs_3_.refs_2_), custom_call_target="tpu_custom_call" | custom-call | flops 1073741824 | bytes 8388608 | tf_op jit(solution)/shard_map/project/pallas_call | solution.py:548
  187.1 4.0 %arrange_pages.1 = bf16[8,128,2,1024]{3,2,1,0:T(2,128)(2,1)} custom-call(s32[8]{0:T(128)} %page_after.1, s32[4]{0:T(128)} %bitcast.27, bf16[8,128,2,1024]{3,2,1,0:T(2,128)(2,1)} %kv_ref.7, bf16[128,2,1024]{2,1,0:T(2,128)(2,1)} %copy-done.5, bf16[128,2,1024]{2,1,0:T(2,128)(2,1)} %copy-done.6, bf16[128,2,1024]{2,1,0:T(2,128)(2,1)} %copy-done.7, ...), custom_call_target="tpu_custom_call" | custom-call | tf_op jit(solution)/shard_map/arrange_pages/pallas_call | solution.py:159
  192.6 4.2 %collective-permute-start.16 = (bf16[16,4096]{1,0:T(8,128)(2,1)S(1)}, bf16[16,4096]{1,0:T(8,128)(2,1)S(1)}, u32[]{:S(2)}, u32[]{:S(2)}) collective-permute-start(bf16[16,4096]{1,0:T(8,128)(2,1)S(1)} %get-tuple-element.53), channel_id=1, source_target_pairs={{0,12},{1,13},{2,14},{3,15},{4,8},{5,9},{6,10},{7,11},{8,4},{9,5},... | collective-permute-start | bytes 393224 | tf_op jit(solution)/shard_map/ppermute | solution.py:31
  200.0 10.0 %collective-permute-done.7 = bf16[64,4096]{1,0:T(8,128)(2,1)} collective-permute-done((bf16[64,4096]{1,0:T(8,128)(2,1)}, bf16[64,4096]{1,0:T(8,128)(2,1)}, u32[]{:S(2)}, u32[]{:S(2)}) %collective-permute-start.7) | collective-permute-done | bytes 524320 | tf_op jit(solution)/shard_map/ppermute | solution.py:31
  211.3 8.6 %collective-permute-done.17 = bf16[64,4096]{1,0:T(8,128)(2,1)} collective-permute-done((bf16[64,4096]{1,0:T(8,128)(2,1)}, bf16[64,4096]{1,0:T(8,128)(2,1)}, u32[]{:S(2)}, u32[]{:S(2)}) %collective-permute-start.17) | collective-permute-done | bytes 524320 | tf_op jit(solution)/shard_map/ppermute | solution.py:31
  219.8 4.0 %collective-permute-start.6 = (bf16[16,4096]{1,0:T(8,128)(2,1)S(1)}, bf16[16,4096]{1,0:T(8,128)(2,1)S(1)}, u32[]{:S(2)}, u32[]{:S(2)}) collective-permute-start(bf16[16,4096]{1,0:T(8,128)(2,1)S(1)} %get-tuple-element.47), channel_id=1, source_target_pairs={{0,12},{1,13},{2,14},{3,15},{4,8},{5,9},{6,10},{7,11},{8,4},{9,5},... | collective-permute-start | bytes 393224 | tf_op jit(solution)/shard_map/ppermute | solution.py:31
  225.7 3.8 %collective-permute-start.10 = (bf16[16,4096]{1,0:T(8,128)(2,1)S(1)}, bf16[16,4096]{1,0:T(8,128)(2,1)S(1)}, u32[]{:S(2)}, u32[]{:S(2)}) collective-permute-start(bf16[16,4096]{1,0:T(8,128)(2,1)S(1)} %get-tuple-element.50), channel_id=1, source_target_pairs={{0,12},{1,13},{2,14},{3,15},{4,8},{5,9},{6,10},{7,11},{8,4},{9,5},... | collective-permute-start | bytes 393224 | tf_op jit(solution)/shard_map/ppermute | solution.py:31
  232.2 7.3 %collective-permute-done.5 = bf16[16,4096]{1,0:T(8,128)(2,1)S(1)} collective-permute-done((bf16[16,4096]{1,0:T(8,128)(2,1)S(1)}, bf16[16,4096]{1,0:T(8,128)(2,1)S(1)}, u32[]{:S(2)}, u32[]{:S(2)}) %collective-permute-start.5) | collective-permute-done | bytes 131104 | tf_op jit(solution)/shard_map/ppermute | solution.py:31
  239.6 11.1 %collective-permute-done.9 = bf16[16,4096]{1,0:T(8,128)(2,1)S(1)} collective-permute-done((bf16[16,4096]{1,0:T(8,128)(2,1)S(1)}, bf16[16,4096]{1,0:T(8,128)(2,1)S(1)}, u32[]{:S(2)}, u32[]{:S(2)}) %collective-permute-start.9) | collective-permute-done | bytes 131104 | tf_op jit(solution)/shard_map/ppermute | solution.py:31
  250.8 4.7 %collective-permute-done.19 = bf16[16,4096]{1,0:T(8,128)(2,1)S(1)} collective-permute-done((bf16[16,4096]{1,0:T(8,128)(2,1)S(1)}, bf16[16,4096]{1,0:T(8,128)(2,1)S(1)}, u32[]{:S(2)}, u32[]{:S(2)}) %collective-permute-start.19) | collective-permute-done | bytes 131104 | tf_op jit(solution)/shard_map/ppermute | solution.py:31
  (95 shorter events, 41.5 us)
Async XLA Ops:
  11.8 34.9 %all-to-all-start.2 = ((bf16[8,5,128,2,128]{4,3,2,1,0:T(2,128)(2,1)}), bf16[8,5,128,2,128]{4,3,2,1,0:T(2,128)(2,1)S(1)}, u32[]{:S(2)}, u32[]{:S(2)}) async-start(bf16[8,5,128,2,128]{4,3,2,1,0:T(2,128)(2,1)} %split_heads.3), calls=%async_computation.2 | async-start | bytes 5242880 | tf_op jit(solution)/shard_map/all_to_all | solution.py:578
  15.4 118.9 %collective-permute-start.2 = (bf16[512,8192]{1,0:T(8,128)(2,1)}, bf16[512,8192]{1,0:T(8,128)(2,1)}, u32[]{:S(2)}, u32[]{:S(2)}) collective-permute-start(bf16[512,8192]{1,0:T(8,128)(2,1)} %refs_1_.3), channel_id=1, source_target_pairs={{0,1},{1,0},{2,3},{3,2},{4,5},{5,4},{6,7},{7,6},{8,9},{9,8},{10,11... | collective-permute-start | bytes 25165832 | tf_op jit(solution)/shard_map/ppermute | solution.py:31
  46.7 50.8 %all-to-all-start.1 = ((bf16[8,3,128,2,128]{4,3,2,1,0:T(2,128)(2,1)}), bf16[8,3,128,2,128]{4,3,2,1,0:T(2,128)(2,1)}, u32[]{:S(2)}, u32[]{:S(2)}) async-start(bf16[8,3,128,2,128]{4,3,2,1,0:T(2,128)(2,1)} %split_heads.2), calls=%async_computation.1 | async-start | bytes 3145728 | tf_op jit(solution)/shard_map/all_to_all | solution.py:578
  106.8 16.7 %collective-permute-start.12 = (bf16[1072,128]{1,0:T(8,128)(2,1)S(1)}, bf16[1072,128]{1,0:T(8,128)(2,1)S(1)}, u32[]{:S(2)}, u32[]{:S(2)}) collective-permute-start(bf16[1072,128]{1,0:T(8,128)(2,1)S(1)} %get-tuple-element.44), channel_id=1, source_target_pairs={{0,1},{1,9},{2,3},{3,11},{4,5},{5,13},{6,7},{7,15},{8,0},{9,8},{10... | collective-permute-start | bytes 823304 | tf_op jit(solution)/shard_map/ppermute | solution.py:31
  107.2 18.9 %collective-permute-start.11 = (bf16[1072,128]{1,0:T(8,128)(2,1)S(1)}, bf16[1072,128]{1,0:T(8,128)(2,1)S(1)}, u32[]{:S(2)}, u32[]{:S(2)}) collective-permute-start(bf16[1072,128]{1,0:T(8,128)(2,1)S(1)} %get-tuple-element.45), channel_id=1, source_target_pairs={{0,0},{1,8},{2,2},{3,10},{4,4},{5,12},{6,6},{7,14},{8,1},{9,9},{10... | collective-permute-start | bytes 823304 | tf_op jit(solution)/shard_map/ppermute | solution.py:31
  117.9 16.4 %collective-permute-start.1 = (bf16[1072,128]{1,0:T(8,128)(2,1)S(1)}, bf16[1072,128]{1,0:T(8,128)(2,1)S(1)}, u32[]{:S(2)}, u32[]{:S(2)}) collective-permute-start(bf16[1072,128]{1,0:T(8,128)(2,1)S(1)} %get-tuple-element.42), channel_id=1, source_target_pairs={{0,1},{1,9},{2,3},{3,11},{4,5},{5,13},{6,7},{7,15},{8,0},{9,8},{10... | collective-permute-start | bytes 823304 | tf_op jit(solution)/shard_map/ppermute | solution.py:31
  121.9 20.2 %collective-permute-start = (bf16[1072,128]{1,0:T(8,128)(2,1)}, bf16[1072,128]{1,0:T(8,128)(2,1)S(1)}, u32[]{:S(2)}, u32[]{:S(2)}) collective-permute-start(bf16[1072,128]{1,0:T(8,128)(2,1)} %get-tuple-element.43), channel_id=1, source_target_pairs={{0,0},{1,8},{2,2},{3,10},{4,4},{5,12},{6,6},{7,14},{8,1},{9,9},{10... | collective-permute-start | bytes 823304 | tf_op jit(solution)/shard_map/ppermute | solution.py:31
  123.5 62.8 %collective-permute-start.21 = (bf16[128,2,1024]{2,1,0:T(2,128)(2,1)}, bf16[128,2,1024]{2,1,0:T(2,128)(2,1)S(1)}, u32[]{:S(2)}, u32[]{:S(2)}) collective-permute-start(bf16[128,2,1024]{2,1,0:T(2,128)(2,1)} %get-tuple-element.18.after_ref), channel_id=1, source_target_pairs={{0,1},{1,2},{2,3},{3,4},{4,5},{5,6},{6,7},{7,8},{8,9},{9,10},{10,1... | collective-permute-start | bytes 1572872 | tf_op jit(solution)/shard_map/ppermute | solution.py:31
  126.1 57.5 %collective-permute-start.22 = (bf16[128,2,1024]{2,1,0:T(2,128)(2,1)}, bf16[128,2,1024]{2,1,0:T(2,128)(2,1)S(1)}, u32[]{:S(2)}, u32[]{:S(2)}) collective-permute-start(bf16[128,2,1024]{2,1,0:T(2,128)(2,1)} %get-tuple-element.31), channel_id=1, source_target_pairs={{0,2},{1,3},{2,4},{3,5},{4,6},{5,7},{6,8},{7,9},{8,10},{9,11},{10,... | collective-permute-start | bytes 1572872 | tf_op jit(solution)/shard_map/ppermute | solution.py:31
  134.3 49.9 %collective-permute-start.23 = (bf16[128,2,1024]{2,1,0:T(2,128)(2,1)}, bf16[128,2,1024]{2,1,0:T(2,128)(2,1)S(1)}, u32[]{:S(2)}, u32[]{:S(2)}) collective-permute-start(bf16[128,2,1024]{2,1,0:T(2,128)(2,1)} %get-tuple-element.32), channel_id=1, source_target_pairs={{0,3},{1,4},{2,5},{3,6},{4,7},{5,8},{6,9},{7,10},{8,11},{9,12},{10... | collective-permute-start | bytes 1572872 | tf_op jit(solution)/shard_map/ppermute | solution.py:31
  134.4 51.3 %collective-permute-start.24 = (bf16[128,2,1024]{2,1,0:T(2,128)(2,1)}, bf16[128,2,1024]{2,1,0:T(2,128)(2,1)S(1)}, u32[]{:S(2)}, u32[]{:S(2)}) collective-permute-start(bf16[128,2,1024]{2,1,0:T(2,128)(2,1)} %get-tuple-element.33), channel_id=1, source_target_pairs={{0,4},{1,5},{2,6},{3,7},{4,8},{5,9},{6,10},{7,11},{8,12},{9,13},{1... | collective-permute-start | bytes 1572872 | tf_op jit(solution)/shard_map/ppermute | solution.py:31
  142.1 49.0 %collective-permute-start.13 = (bf16[64,4096]{1,0:T(8,128)(2,1)}, bf16[64,4096]{1,0:T(8,128)(2,1)}, u32[]{:S(2)}, u32[]{:S(2)}) collective-permute-start(bf16[64,4096]{1,0:T(8,128)(2,1)} %get-tuple-element.27), channel_id=1, source_target_pairs={{0,2},{1,3},{2,0},{3,1},{4,6},{5,7},{6,4},{7,5},{8,10},{9,11},{10,... | collective-permute-start | bytes 1572872 | tf_op jit(solution)/shard_map/ppermute | solution.py:31
  183.6 15.2 %collective-permute-start.3 = (bf16[64,4096]{1,0:T(8,128)(2,1)}, bf16[64,4096]{1,0:T(8,128)(2,1)}, u32[]{:S(2)}, u32[]{:S(2)}) collective-permute-start(bf16[64,4096]{1,0:T(8,128)(2,1)} %get-tuple-element.22), channel_id=1, source_target_pairs={{0,2},{1,3},{2,0},{3,1},{4,6},{5,7},{6,4},{7,5},{8,10},{9,11},{10,... | collective-permute-start | bytes 1572872 | tf_op jit(solution)/shard_map/ppermute | solution.py:31
  184.3 25.7 %collective-permute-start.7 = (bf16[64,4096]{1,0:T(8,128)(2,1)}, bf16[64,4096]{1,0:T(8,128)(2,1)}, u32[]{:S(2)}, u32[]{:S(2)}) collective-permute-start(bf16[64,4096]{1,0:T(8,128)(2,1)} %get-tuple-element.25), channel_id=1, source_target_pairs={{0,2},{1,3},{2,0},{3,1},{4,6},{5,7},{6,4},{7,5},{8,10},{9,11},{10,... | collective-permute-start | bytes 1572872 | tf_op jit(solution)/shard_map/ppermute | solution.py:31
  185.7 34.1 %collective-permute-start.17 = (bf16[64,4096]{1,0:T(8,128)(2,1)}, bf16[64,4096]{1,0:T(8,128)(2,1)}, u32[]{:S(2)}, u32[]{:S(2)}) collective-permute-start(bf16[64,4096]{1,0:T(8,128)(2,1)} %get-tuple-element.30.refs_4_), channel_id=1, source_target_pairs={{0,2},{1,3},{2,0},{3,1},{4,6},{5,7},{6,4},{7,5},{8,10},{9,11},{10,... | collective-permute-start | bytes 1572872 | tf_op jit(solution)/shard_map/ppermute | solution.py:31
  192.5 32.5 %collective-permute-start.14 = (bf16[16,4096]{1,0:T(8,128)(2,1)S(1)}, bf16[16,4096]{1,0:T(8,128)(2,1)S(1)}, u32[]{:S(2)}, u32[]{:S(2)}) collective-permute-start(bf16[16,4096]{1,0:T(8,128)(2,1)S(1)} %get-tuple-element.52), channel_id=1, source_target_pairs={{0,4},{1,5},{2,6},{3,7},{4,0},{5,1},{6,2},{7,3},{8,12},{9,13},{10,... | collective-permute-start | bytes 393224 | tf_op jit(solution)/shard_map/ppermute | solution.py:31
  192.6 32.5 %collective-permute-start.16 = (bf16[16,4096]{1,0:T(8,128)(2,1)S(1)}, bf16[16,4096]{1,0:T(8,128)(2,1)S(1)}, u32[]{:S(2)}, u32[]{:S(2)}) collective-permute-start(bf16[16,4096]{1,0:T(8,128)(2,1)S(1)} %get-tuple-element.53), channel_id=1, source_target_pairs={{0,12},{1,13},{2,14},{3,15},{4,8},{5,9},{6,10},{7,11},{8,4},{9,5},... | collective-permute-start | bytes 393224 | tf_op jit(solution)/shard_map/ppermute | solution.py:31
  198.8 26.9 %collective-permute-start.15 = (bf16[16,4096]{1,0:T(8,128)(2,1)S(1)}, bf16[16,4096]{1,0:T(8,128)(2,1)S(1)}, u32[]{:S(2)}, u32[]{:S(2)}) collective-permute-start(bf16[16,4096]{1,0:T(8,128)(2,1)S(1)} %get-tuple-element.54), channel_id=1, source_target_pairs={{0,8},{1,9},{2,10},{3,11},{4,12},{5,13},{6,14},{7,15},{8,0},{9,1},... | collective-permute-start | bytes 393224 | tf_op jit(solution)/shard_map/ppermute | solution.py:31
  210.0 19.6 %collective-permute-start.4 = (bf16[16,4096]{1,0:T(8,128)(2,1)S(1)}, bf16[16,4096]{1,0:T(8,128)(2,1)S(1)}, u32[]{:S(2)}, u32[]{:S(2)}) collective-permute-start(bf16[16,4096]{1,0:T(8,128)(2,1)S(1)} %get-tuple-element.46), channel_id=1, source_target_pairs={{0,4},{1,5},{2,6},{3,7},{4,0},{5,1},{6,2},{7,3},{8,12},{9,13},{10,... | collective-permute-start | bytes 393224 | tf_op jit(solution)/shard_map/ppermute | solution.py:31
  225.1 14.4 %collective-permute-start.5 = (bf16[16,4096]{1,0:T(8,128)(2,1)S(1)}, bf16[16,4096]{1,0:T(8,128)(2,1)S(1)}, u32[]{:S(2)}, u32[]{:S(2)}) collective-permute-start(bf16[16,4096]{1,0:T(8,128)(2,1)S(1)} %get-tuple-element.48), channel_id=1, source_target_pairs={{0,8},{1,9},{2,10},{3,11},{4,12},{5,13},{6,14},{7,15},{8,0},{9,1},... | collective-permute-start | bytes 393224 | tf_op jit(solution)/shard_map/ppermute | solution.py:31
  225.2 14.3 %collective-permute-start.8 = (bf16[16,4096]{1,0:T(8,128)(2,1)S(1)}, bf16[16,4096]{1,0:T(8,128)(2,1)S(1)}, u32[]{:S(2)}, u32[]{:S(2)}) collective-permute-start(bf16[16,4096]{1,0:T(8,128)(2,1)S(1)} %get-tuple-element.49), channel_id=1, source_target_pairs={{0,4},{1,5},{2,6},{3,7},{4,0},{5,1},{6,2},{7,3},{8,12},{9,13},{10,... | collective-permute-start | bytes 393224 | tf_op jit(solution)/shard_map/ppermute | solution.py:31
  229.6 21.1 %collective-permute-start.9 = (bf16[16,4096]{1,0:T(8,128)(2,1)S(1)}, bf16[16,4096]{1,0:T(8,128)(2,1)S(1)}, u32[]{:S(2)}, u32[]{:S(2)}) collective-permute-start(bf16[16,4096]{1,0:T(8,128)(2,1)S(1)} %get-tuple-element.51), channel_id=1, source_target_pairs={{0,8},{1,9},{2,10},{3,11},{4,12},{5,13},{6,14},{7,15},{8,0},{9,1},... | collective-permute-start | bytes 393224 | tf_op jit(solution)/shard_map/ppermute | solution.py:31
  229.7 21.1 %collective-permute-start.18 = (bf16[16,4096]{1,0:T(8,128)(2,1)S(1)}, bf16[16,4096]{1,0:T(8,128)(2,1)S(1)}, u32[]{:S(2)}, u32[]{:S(2)}) collective-permute-start(bf16[16,4096]{1,0:T(8,128)(2,1)S(1)} %get-tuple-element.55), channel_id=1, source_target_pairs={{0,4},{1,5},{2,6},{3,7},{4,0},{5,1},{6,2},{7,3},{8,12},{9,13},{10,... | collective-permute-start | bytes 393224 | tf_op jit(solution)/shard_map/ppermute | solution.py:31
  239.5 15.9 %collective-permute-start.19 = (bf16[16,4096]{1,0:T(8,128)(2,1)S(1)}, bf16[16,4096]{1,0:T(8,128)(2,1)S(1)}, u32[]{:S(2)}, u32[]{:S(2)}) collective-permute-start(bf16[16,4096]{1,0:T(8,128)(2,1)S(1)} %get-tuple-element.57), channel_id=1, source_target_pairs={{0,8},{1,9},{2,10},{3,11},{4,12},{5,13},{6,14},{7,15},{8,0},{9,1},... | collective-permute-start | bytes 393224 | tf_op jit(solution)/shard_map/ppermute | solution.py:31
  (18 other events, 212.7 us)
